TPU v7x, 256 devices: a whole 4x4x8 slice. The times are simulated.
256 devices in a mesh: cuts: 64 (over x, y, z_lo), frame: 4 (over z_hi, core).
Axes of the slice: x: 4, y: 4, z: 8 (z_hi: 2, z_lo: 4; z = z_hi * 4 + z_lo), core: 2. Of those that a mesh axis runs over, the one named last changes fastest.
Arguments:
- basis: bfloat16 [2, 32, 128, 4, 256], P(None, None, 'cuts', 'frame'), may hold values from -6 to 6
- coil_maps: bfloat16 [2, 12, 128, 4, 256], P(None, None, 'cuts', 'frame'), may hold values from -3 to 3
- factors: bfloat16 [2, 32, 64], P(None, None, 'frame'), may hold values from -0.75 to 0.75
- lines: int32 [64, 128], P(None, 'cuts'), may hold values from 0 to 511
- kdata: bfloat16 [2, 64, 128, 12, 4], P(None, None, 'cuts', None, 'frame'), may hold values from -6 to 6
Outputs:
- basis_grad: float32 [2, 32, 128, 4, 256], P(None, None, 'cuts', 'frame')
- factor_grad: float32 [2, 32, 64], P(None, None, 'frame')
Inputs may be any that keep to these rules, and one draw needn't show every extreme that they name: lines[t, j] = (ky - (j // 2) * 4) * 128 + kz for a position (ky, kz) sampled in frame t whose ky lies in the rows (j // 2) * 4 to (j // 2 + 1) * 4 - 1; positions may repeat over frames.
All inputs are finite; a program needn't handle non-finite values.
Results may differ from a plain program's by a relative error of at most 0.011.
Values may be sent and summed in bfloat16 or wider, within the bound.
A program may use at most 64 MiB of HBM per device.

v0:
```python
import math

import jax
import jax.numpy as jnp
from jax import lax
from jax.sharding import PartitionSpec as P

HIGH = lax.Precision.HIGHEST


def twiddle(product, size):
    angle = product.astype(jnp.float32) * (2.0 * math.pi / size)
    factor = 1.0 / math.sqrt(size)
    return (
        (jnp.cos(angle) * factor).astype(jnp.bfloat16),
        (jnp.sin(angle) * factor).astype(jnp.bfloat16),
    )


def dft_table(size, inverse):
    index = jnp.arange(size, dtype=jnp.int32)
    product = index[:, None] * index[None, :] % size
    cosine, sine = twiddle(product, size)
    imag = sine if inverse else -sine
    return jnp.stack([jnp.stack([cosine, imag]), jnp.stack([-imag, cosine])])


def body(basis, coil_maps, factors, lines, kdata):
    n_cuts = lax.axis_size("cuts")
    slab = basis.shape[2]
    readout = basis.shape[3]
    width = basis.shape[4]
    depth = slab * n_cuts
    ky_rows = width // n_cuts
    lines_dev = lines.shape[1]
    scale = 1.0 / math.sqrt(
        coil_maps.shape[1] * lines_dev * n_cuts * readout * lax.axis_size("frame")
    )
    fwd_y = dft_table(width, False)
    inv_y = dft_table(width, True)
    every = lax.all_gather(factors, "frame", axis=2, tiled=True)
    frames = every.shape[2]
    v_re = every[0]
    v_im = every[1]
    v_re32 = v_re.astype(jnp.float32)
    v_im32 = v_im.astype(jnp.float32)
    b_re = basis[0].astype(jnp.float32)
    b_im = basis[1].astype(jnp.float32)

    def forward_hybrid(maps):
        m_re = maps[0].astype(jnp.float32)[None]
        m_im = maps[1].astype(jnp.float32)[None]
        image = jnp.stack([m_re * b_re - m_im * b_im, m_re * b_im + m_im * b_re]).astype(
            jnp.bfloat16
        )
        return jnp.einsum(
            "plzxy,pqwy->qlzxw", image, fwd_y, preferred_element_type=jnp.float32
        ).astype(jnp.bfloat16)

    def finish(back, maps, grad_acc):
        imgrad = jnp.einsum("plzxw,pqyw->qlzxy", back, inv_y, preferred_element_type=jnp.float32)
        m_re = maps[0].astype(jnp.float32)[None]
        m_im = maps[1].astype(jnp.float32)[None]
        g_re = imgrad[0]
        g_im = imgrad[1]
        return grad_acc + jnp.stack([m_re * g_re + m_im * g_im, m_re * g_im - m_im * g_re])

    fwd_z = dft_table(depth, False)
    inv_z = dft_table(depth, True).astype(jnp.float32)
    cells = depth * ky_rows
    cell_of = lines % depth * ky_rows + lines // depth
    onehot = (cell_of[:, :, None] == jnp.arange(cells, dtype=jnp.int32)[None, None, :]).astype(
        jnp.bfloat16
    )
    onehot32 = onehot.astype(jnp.float32)

    def coil_step(carry, inputs):
        grad_acc, factor_acc = carry
        maps, data = inputs
        hybrid = forward_hybrid(maps)
        moved = lax.all_to_all(hybrid, "cuts", split_axis=4, concat_axis=2, tiled=True)
        kspace = jnp.einsum("plzxr,pqkz->qlxkr", moved, fwd_z, preferred_element_type=jnp.float32)
        kspace = kspace.reshape(2, kspace.shape[1], readout, cells)
        k_re = kspace[0]
        k_im = kspace[1]
        mixed_re = jnp.einsum("lxc,lt->xtc", k_re, v_re32, precision=HIGH) - jnp.einsum(
            "lxc,lt->xtc", k_im, v_im32, precision=HIGH
        )
        mixed_im = jnp.einsum("lxc,lt->xtc", k_re, v_im32, precision=HIGH) + jnp.einsum(
            "lxc,lt->xtc", k_im, v_re32, precision=HIGH
        )
        pred_re = jnp.einsum("tsc,xtc->tsx", onehot32, mixed_re, precision=HIGH)
        pred_im = jnp.einsum("tsc,xtc->tsx", onehot32, mixed_im, precision=HIGH)
        resid = (jnp.stack([pred_re, pred_im]) - data.astype(jnp.float32)).astype(jnp.bfloat16)
        spread = jnp.einsum("qtsx,tsc->qxtc", resid, onehot, preferred_element_type=jnp.float32)
        e_re = spread[0]
        e_im = spread[1]
        gv_re = jnp.einsum("lxc,xtc->lt", k_re, e_re, precision=HIGH) + jnp.einsum(
            "lxc,xtc->lt", k_im, e_im, precision=HIGH
        )
        gv_im = jnp.einsum("lxc,xtc->lt", k_re, e_im, precision=HIGH) - jnp.einsum(
            "lxc,xtc->lt", k_im, e_re, precision=HIGH
        )
        kg_re = jnp.einsum("xtc,lt->lxc", e_re, v_re32, precision=HIGH) + jnp.einsum(
            "xtc,lt->lxc", e_im, v_im32, precision=HIGH
        )
        kg_im = jnp.einsum("xtc,lt->lxc", e_im, v_re32, precision=HIGH) - jnp.einsum(
            "xtc,lt->lxc", e_re, v_im32, precision=HIGH
        )
        kgrad = jnp.stack([kg_re, kg_im]).reshape(2, kg_re.shape[0], readout, depth, ky_rows)
        zgrad = jnp.einsum("plxkr,pqzk->qlzxr", kgrad, inv_z, precision=HIGH).astype(jnp.bfloat16)
        back = lax.all_to_all(zgrad, "cuts", split_axis=2, concat_axis=4, tiled=True)
        return ((finish(back, maps, grad_acc), factor_acc + jnp.stack([gv_re, gv_im])), None)

    start_state = (
        jnp.zeros(basis.shape, jnp.float32),
        jnp.zeros((2, basis.shape[1], frames), jnp.float32),
    )
    inputs = (coil_maps.transpose(1, 0, 2, 3, 4), kdata.transpose(3, 0, 1, 2, 4))
    (grad_acc, factor_acc), unused = lax.scan(coil_step, start_state, inputs)
    shared = lax.psum_scatter(factor_acc * scale, "frame", scatter_dimension=2, tiled=True)
    factor_grad = lax.psum(shared, "cuts")
    return (grad_acc, factor_grad)


def solution(mesh):
    placed = (
        P(None, None, "cuts", "frame", None),
        P(None, None, "cuts", "frame", None),
        P(None, None, "frame"),
        P(None, "cuts"),
        P(None, None, "cuts", None, "frame"),
    )
    return jax.shard_map(
        body,
        mesh=mesh,
        in_specs=placed,
        out_specs=(P(None, None, "cuts", "frame", None), P(None, None, "frame")),
        check_vma=False,
    )
```

profile of v0, /device:TPU:0, one launch (start us, length us, event | category | flops | bytes accessed | tf_op | source)
XLA Modules:
  0.0 969.2 jit_solution(9303458574597565671)
XLA Ops:
  12.5 9.3 all_gather.3
  23.5 538.5 %while.15 = (s32[]{:T(128)}, f32[2,32,2,1,256]{4,1,0,2,3:T(8,128)S(1)}, f32[2,32,64]{2,1,0:T(8,128)S(1)}, bf16[12,2,2,1,256]{4,2,3,1,0:T(2,128)(2,1)S(1)}, f32[3...) while((s32[]{:T(128)}, ...), condition=%wide.region_1.2_spmd.clone.clone.clone, body=%wide.region_0.1_spmd.clone.clone.clone.sunk | while | flops 338577408 | bytes 9754888 | solution.py:120
  24.8 10.3 %all-to-all-start = ((bf16[64,2,256]{2,1,0:T(2,128)(2,1)}), bf16[64,2,256]{2,1,0:T(2,128)(2,1)S(1)}, u32[]{:S(2)}, u32[]{:S(2)}) async-start(bf16[64,2,256]{2,1,0:T(2,128)(2,1)} %reshape.531), calls=%async_computation | async-start | bytes 131072 | tf_op jit(solution)/shard_map/while/body/eval_jaxpr/all_to_all | solution.py:81
  35.1 10.0 %all-to-all-done = bf16[64,2,256]{2,1,0:T(2,128)(2,1)S(1)} async-done(((bf16[64,2,256]{2,1,0:T(2,128)(2,1)}), bf16[64,2,256]{2,1,0:T(2,128)(2,1)S(1)}, u32[]{:S(2)}, u32[]{:S(2)}) %all-to-all-start) | async-done | bytes 65568 | tf_op jit(solution)/shard_map/while/body/eval_jaxpr/all_to_all | solution.py:81
  58.0 4.6 all-to-all-start.1
  62.7 10.0 %all-to-all-done.1 = bf16[64,2,256]{2,1,0:T(2,128)(2,1)S(1)} async-done(((bf16[64,2,256]{2,1,0:T(2,128)(2,1)}), bf16[64,2,256]{2,1,0:T(2,128)(2,1)S(1)}, u32[]{:S(2)}, u32[]{:S(2)}) %all-to-all-start.1) | async-done | bytes 65568 | tf_op jit(solution)/shard_map/while/body/eval_jaxpr/all_to_all | solution.py:112
  74.8 4.6 all-to-all-start
  79.5 10.0 %all-to-all-done = bf16[64,2,256]{2,1,0:T(2,128)(2,1)S(1)} async-done(((bf16[64,2,256]{2,1,0:T(2,128)(2,1)}), bf16[64,2,256]{2,1,0:T(2,128)(2,1)S(1)}, u32[]{:S(2)}, u32[]{:S(2)}) %all-to-all-start) | async-done | bytes 65568 | tf_op jit(solution)/shard_map/while/body/eval_jaxpr/all_to_all | solution.py:81
  107.0 10.0 %all-to-all-done.1 = bf16[64,2,256]{2,1,0:T(2,128)(2,1)S(1)} async-done(((bf16[64,2,256]{2,1,0:T(2,128)(2,1)}), bf16[64,2,256]{2,1,0:T(2,128)(2,1)S(1)}, u32[]{:S(2)}, u32[]{:S(2)}) %all-to-all-start.1) | async-done | bytes 65568 | tf_op jit(solution)/shard_map/while/body/eval_jaxpr/all_to_all | solution.py:112
  123.8 10.0 %all-to-all-done = bf16[64,2,256]{2,1,0:T(2,128)(2,1)S(1)} async-done(((bf16[64,2,256]{2,1,0:T(2,128)(2,1)}), bf16[64,2,256]{2,1,0:T(2,128)(2,1)S(1)}, u32[]{:S(2)}, u32[]{:S(2)}) %all-to-all-start) | async-done | bytes 65568 | tf_op jit(solution)/shard_map/while/body/eval_jaxpr/all_to_all | solution.py:81
  151.3 10.0 %all-to-all-done.1 = bf16[64,2,256]{2,1,0:T(2,128)(2,1)S(1)} async-done(((bf16[64,2,256]{2,1,0:T(2,128)(2,1)}), bf16[64,2,256]{2,1,0:T(2,128)(2,1)S(1)}, u32[]{:S(2)}, u32[]{:S(2)}) %all-to-all-start.1) | async-done | bytes 65568 | tf_op jit(solution)/shard_map/while/body/eval_jaxpr/all_to_all | solution.py:112
  168.2 10.0 %all-to-all-done = bf16[64,2,256]{2,1,0:T(2,128)(2,1)S(1)} async-done(((bf16[64,2,256]{2,1,0:T(2,128)(2,1)}), bf16[64,2,256]{2,1,0:T(2,128)(2,1)S(1)}, u32[]{:S(2)}, u32[]{:S(2)}) %all-to-all-start) | async-done | bytes 65568 | tf_op jit(solution)/shard_map/while/body/eval_jaxpr/all_to_all | solution.py:81
  195.7 10.0 %all-to-all-done.1 = bf16[64,2,256]{2,1,0:T(2,128)(2,1)S(1)} async-done(((bf16[64,2,256]{2,1,0:T(2,128)(2,1)}), bf16[64,2,256]{2,1,0:T(2,128)(2,1)S(1)}, u32[]{:S(2)}, u32[]{:S(2)}) %all-to-all-start.1) | async-done | bytes 65568 | tf_op jit(solution)/shard_map/while/body/eval_jaxpr/all_to_all | solution.py:112
  212.5 10.0 %all-to-all-done = bf16[64,2,256]{2,1,0:T(2,128)(2,1)S(1)} async-done(((bf16[64,2,256]{2,1,0:T(2,128)(2,1)}), bf16[64,2,256]{2,1,0:T(2,128)(2,1)S(1)}, u32[]{:S(2)}, u32[]{:S(2)}) %all-to-all-start) | async-done | bytes 65568 | tf_op jit(solution)/shard_map/while/body/eval_jaxpr/all_to_all | solution.py:81
  240.0 10.0 %all-to-all-done.1 = bf16[64,2,256]{2,1,0:T(2,128)(2,1)S(1)} async-done(((bf16[64,2,256]{2,1,0:T(2,128)(2,1)}), bf16[64,2,256]{2,1,0:T(2,128)(2,1)S(1)}, u32[]{:S(2)}, u32[]{:S(2)}) %all-to-all-start.1) | async-done | bytes 65568 | tf_op jit(solution)/shard_map/while/body/eval_jaxpr/all_to_all | solution.py:112
  256.8 10.0 %all-to-all-done = bf16[64,2,256]{2,1,0:T(2,128)(2,1)S(1)} async-done(((bf16[64,2,256]{2,1,0:T(2,128)(2,1)}), bf16[64,2,256]{2,1,0:T(2,128)(2,1)S(1)}, u32[]{:S(2)}, u32[]{:S(2)}) %all-to-all-start) | async-done | bytes 65568 | tf_op jit(solution)/shard_map/while/body/eval_jaxpr/all_to_all | solution.py:81
  284.4 10.0 %all-to-all-done.1 = bf16[64,2,256]{2,1,0:T(2,128)(2,1)S(1)} async-done(((bf16[64,2,256]{2,1,0:T(2,128)(2,1)}), bf16[64,2,256]{2,1,0:T(2,128)(2,1)S(1)}, u32[]{:S(2)}, u32[]{:S(2)}) %all-to-all-start.1) | async-done | bytes 65568 | tf_op jit(solution)/shard_map/while/body/eval_jaxpr/all_to_all | solution.py:112
  301.2 10.0 %all-to-all-done = bf16[64,2,256]{2,1,0:T(2,128)(2,1)S(1)} async-done(((bf16[64,2,256]{2,1,0:T(2,128)(2,1)}), bf16[64,2,256]{2,1,0:T(2,128)(2,1)S(1)}, u32[]{:S(2)}, u32[]{:S(2)}) %all-to-all-start) | async-done | bytes 65568 | tf_op jit(solution)/shard_map/while/body/eval_jaxpr/all_to_all | solution.py:81
  328.7 10.4 %all-to-all-done.1 = bf16[64,2,256]{2,1,0:T(2,128)(2,1)S(1)} async-done(((bf16[64,2,256]{2,1,0:T(2,128)(2,1)}), bf16[64,2,256]{2,1,0:T(2,128)(2,1)S(1)}, u32[]{:S(2)}, u32[]{:S(2)}) %all-to-all-start.1) | async-done | bytes 65568 | tf_op jit(solution)/shard_map/while/body/eval_jaxpr/all_to_all | solution.py:112
  346.0 10.0 %all-to-all-done = bf16[64,2,256]{2,1,0:T(2,128)(2,1)S(1)} async-done(((bf16[64,2,256]{2,1,0:T(2,128)(2,1)}), bf16[64,2,256]{2,1,0:T(2,128)(2,1)S(1)}, u32[]{:S(2)}, u32[]{:S(2)}) %all-to-all-start) | async-done | bytes 65568 | tf_op jit(solution)/shard_map/while/body/eval_jaxpr/all_to_all | solution.py:81
  373.5 10.0 %all-to-all-done.1 = bf16[64,2,256]{2,1,0:T(2,128)(2,1)S(1)} async-done(((bf16[64,2,256]{2,1,0:T(2,128)(2,1)}), bf16[64,2,256]{2,1,0:T(2,128)(2,1)S(1)}, u32[]{:S(2)}, u32[]{:S(2)}) %all-to-all-start.1) | async-done | bytes 65568 | tf_op jit(solution)/shard_map/while/body/eval_jaxpr/all_to_all | solution.py:112
  390.3 10.0 %all-to-all-done = bf16[64,2,256]{2,1,0:T(2,128)(2,1)S(1)} async-done(((bf16[64,2,256]{2,1,0:T(2,128)(2,1)}), bf16[64,2,256]{2,1,0:T(2,128)(2,1)S(1)}, u32[]{:S(2)}, u32[]{:S(2)}) %all-to-all-start) | async-done | bytes 65568 | tf_op jit(solution)/shard_map/while/body/eval_jaxpr/all_to_all | solution.py:81
  417.9 10.0 %all-to-all-done.1 = bf16[64,2,256]{2,1,0:T(2,128)(2,1)S(1)} async-done(((bf16[64,2,256]{2,1,0:T(2,128)(2,1)}), bf16[64,2,256]{2,1,0:T(2,128)(2,1)S(1)}, u32[]{:S(2)}, u32[]{:S(2)}) %all-to-all-start.1) | async-done | bytes 65568 | tf_op jit(solution)/shard_map/while/body/eval_jaxpr/all_to_all | solution.py:112
  434.7 10.0 %all-to-all-done = bf16[64,2,256]{2,1,0:T(2,128)(2,1)S(1)} async-done(((bf16[64,2,256]{2,1,0:T(2,128)(2,1)}), bf16[64,2,256]{2,1,0:T(2,128)(2,1)S(1)}, u32[]{:S(2)}, u32[]{:S(2)}) %all-to-all-start) | async-done | bytes 65568 | tf_op jit(solution)/shard_map/while/body/eval_jaxpr/all_to_all | solution.py:81
  462.2 10.0 %all-to-all-done.1 = bf16[64,2,256]{2,1,0:T(2,128)(2,1)S(1)} async-done(((bf16[64,2,256]{2,1,0:T(2,128)(2,1)}), bf16[64,2,256]{2,1,0:T(2,128)(2,1)S(1)}, u32[]{:S(2)}, u32[]{:S(2)}) %all-to-all-start.1) | async-done | bytes 65568 | tf_op jit(solution)/shard_map/while/body/eval_jaxpr/all_to_all | solution.py:112
  479.0 10.0 %all-to-all-done = bf16[64,2,256]{2,1,0:T(2,128)(2,1)S(1)} async-done(((bf16[64,2,256]{2,1,0:T(2,128)(2,1)}), bf16[64,2,256]{2,1,0:T(2,128)(2,1)S(1)}, u32[]{:S(2)}, u32[]{:S(2)}) %all-to-all-start) | async-done | bytes 65568 | tf_op jit(solution)/shard_map/while/body/eval_jaxpr/all_to_all | solution.py:81
  506.6 10.0 %all-to-all-done.1 = bf16[64,2,256]{2,1,0:T(2,128)(2,1)S(1)} async-done(((bf16[64,2,256]{2,1,0:T(2,128)(2,1)}), bf16[64,2,256]{2,1,0:T(2,128)(2,1)S(1)}, u32[]{:S(2)}, u32[]{:S(2)}) %all-to-all-start.1) | async-done | bytes 65568 | tf_op jit(solution)/shard_map/while/body/eval_jaxpr/all_to_all | solution.py:112
  523.4 10.0 %all-to-all-done = bf16[64,2,256]{2,1,0:T(2,128)(2,1)S(1)} async-done(((bf16[64,2,256]{2,1,0:T(2,128)(2,1)}), bf16[64,2,256]{2,1,0:T(2,128)(2,1)S(1)}, u32[]{:S(2)}, u32[]{:S(2)}) %all-to-all-start) | async-done | bytes 65568 | tf_op jit(solution)/shard_map/while/body/eval_jaxpr/all_to_all | solution.py:81
  546.3 4.8 all-to-all-start.1
  551.1 10.0 %all-to-all-done.1 = bf16[64,2,256]{2,1,0:T(2,128)(2,1)S(1)} async-done(((bf16[64,2,256]{2,1,0:T(2,128)(2,1)}), bf16[64,2,256]{2,1,0:T(2,128)(2,1)S(1)}, u32[]{:S(2)}, u32[]{:S(2)}) %all-to-all-start.1) | async-done | bytes 65568 | tf_op jit(solution)/shard_map/while/body/eval_jaxpr/all_to_all | solution.py:112
  563.6 30.3 %reduce-scatter.4.cloned.1.call-done = f32[16,64]{1,0:T(8,128)} async-done(((f32[64,64]{1,0:T(8,128)}), f32[16,64]{1,0:T(8,128)}) %reduce-scatter.4.cloned.1.call-update) | async-done | bytes 4112
  594.8 366.9 %psum.7 = f32[2,32,16]{2,1,0:T(8,128)S(1)} all-reduce(f32[2,32,16]{2,1,0:T(8,128)S(1)} %copy.183), channel_id=1, replica_groups=mesh['cuts'=64,'frame'=4] {'cuts'}, use_global_device_ids=true, to_apply=%region_3.4 | all-reduce | flops 1024 | bytes 8192 | tf_op jit(solution)/shard_map/psum | solution.py:122
  (617 shorter events, 280.5 us)
Async XLA Ops:
  7.2 586.8 %reduce-scatter.4.cloned.1.call-start = ((), (), s32[]{:S(2)}) async-start(), calls=%async_computation.3 | async-start | bytes 40960
  9.9 0.7 copy-start.4
  10.9 0.8 copy-start
  11.7 0.7 copy-start.3
  21.8 0.7 copy-start.1
  22.6 0.7 copy-start.2
  24.8 20.3 %all-to-all-start = ((bf16[64,2,256]{2,1,0:T(2,128)(2,1)}), bf16[64,2,256]{2,1,0:T(2,128)(2,1)S(1)}, u32[]{:S(2)}, u32[]{:S(2)}) async-start(bf16[64,2,256]{2,1,0:T(2,128)(2,1)} %reshape.531), calls=%async_computation | async-start | bytes 131072 | tf_op jit(solution)/shard_map/while/body/eval_jaxpr/all_to_all | solution.py:81
  58.0 14.6 %all-to-all-start.1 = ((bf16[64,2,256]{2,1,0:T(2,128)(2,1)}), bf16[64,2,256]{2,1,0:T(2,128)(2,1)S(1)}, u32[]{:S(2)}, u32[]{:S(2)}) async-start(bf16[64,2,256]{2,1,0:T(2,128)(2,1)} %reshape.533), calls=%async_computation.1 | async-start | bytes 131072 | tf_op jit(solution)/shard_map/while/body/eval_jaxpr/all_to_all | solution.py:112
  74.8 14.6 %all-to-all-start = ((bf16[64,2,256]{2,1,0:T(2,128)(2,1)}), bf16[64,2,256]{2,1,0:T(2,128)(2,1)S(1)}, u32[]{:S(2)}, u32[]{:S(2)}) async-start(bf16[64,2,256]{2,1,0:T(2,128)(2,1)} %reshape.531), calls=%async_computation | async-start | bytes 131072 | tf_op jit(solution)/shard_map/while/body/eval_jaxpr/all_to_all | solution.py:81
  102.4 14.6 %all-to-all-start.1 = ((bf16[64,2,256]{2,1,0:T(2,128)(2,1)}), bf16[64,2,256]{2,1,0:T(2,128)(2,1)S(1)}, u32[]{:S(2)}, u32[]{:S(2)}) async-start(bf16[64,2,256]{2,1,0:T(2,128)(2,1)} %reshape.533), calls=%async_computation.1 | async-start | bytes 131072 | tf_op jit(solution)/shard_map/while/body/eval_jaxpr/all_to_all | solution.py:112
  119.2 14.6 %all-to-all-start = ((bf16[64,2,256]{2,1,0:T(2,128)(2,1)}), bf16[64,2,256]{2,1,0:T(2,128)(2,1)S(1)}, u32[]{:S(2)}, u32[]{:S(2)}) async-start(bf16[64,2,256]{2,1,0:T(2,128)(2,1)} %reshape.531), calls=%async_computation | async-start | bytes 131072 | tf_op jit(solution)/shard_map/while/body/eval_jaxpr/all_to_all | solution.py:81
  146.7 14.6 %all-to-all-start.1 = ((bf16[64,2,256]{2,1,0:T(2,128)(2,1)}), bf16[64,2,256]{2,1,0:T(2,128)(2,1)S(1)}, u32[]{:S(2)}, u32[]{:S(2)}) async-start(bf16[64,2,256]{2,1,0:T(2,128)(2,1)} %reshape.533), calls=%async_computation.1 | async-start | bytes 131072 | tf_op jit(solution)/shard_map/while/body/eval_jaxpr/all_to_all | solution.py:112
  163.5 14.6 %all-to-all-start = ((bf16[64,2,256]{2,1,0:T(2,128)(2,1)}), bf16[64,2,256]{2,1,0:T(2,128)(2,1)S(1)}, u32[]{:S(2)}, u32[]{:S(2)}) async-start(bf16[64,2,256]{2,1,0:T(2,128)(2,1)} %reshape.531), calls=%async_computation | async-start | bytes 131072 | tf_op jit(solution)/shard_map/while/body/eval_jaxpr/all_to_all | solution.py:81
  191.0 14.6 %all-to-all-start.1 = ((bf16[64,2,256]{2,1,0:T(2,128)(2,1)}), bf16[64,2,256]{2,1,0:T(2,128)(2,1)S(1)}, u32[]{:S(2)}, u32[]{:S(2)}) async-start(bf16[64,2,256]{2,1,0:T(2,128)(2,1)} %reshape.533), calls=%async_computation.1 | async-start | bytes 131072 | tf_op jit(solution)/shard_map/while/body/eval_jaxpr/all_to_all | solution.py:112
  207.9 14.6 %all-to-all-start = ((bf16[64,2,256]{2,1,0:T(2,128)(2,1)}), bf16[64,2,256]{2,1,0:T(2,128)(2,1)S(1)}, u32[]{:S(2)}, u32[]{:S(2)}) async-start(bf16[64,2,256]{2,1,0:T(2,128)(2,1)} %reshape.531), calls=%async_computation | async-start | bytes 131072 | tf_op jit(solution)/shard_map/while/body/eval_jaxpr/all_to_all | solution.py:81
  235.4 14.6 %all-to-all-start.1 = ((bf16[64,2,256]{2,1,0:T(2,128)(2,1)}), bf16[64,2,256]{2,1,0:T(2,128)(2,1)S(1)}, u32[]{:S(2)}, u32[]{:S(2)}) async-start(bf16[64,2,256]{2,1,0:T(2,128)(2,1)} %reshape.533), calls=%async_computation.1 | async-start | bytes 131072 | tf_op jit(solution)/shard_map/while/body/eval_jaxpr/all_to_all | solution.py:112
  252.2 14.6 %all-to-all-start = ((bf16[64,2,256]{2,1,0:T(2,128)(2,1)}), bf16[64,2,256]{2,1,0:T(2,128)(2,1)S(1)}, u32[]{:S(2)}, u32[]{:S(2)}) async-start(bf16[64,2,256]{2,1,0:T(2,128)(2,1)} %reshape.531), calls=%async_computation | async-start | bytes 131072 | tf_op jit(solution)/shard_map/while/body/eval_jaxpr/all_to_all | solution.py:81
  279.7 14.6 %all-to-all-start.1 = ((bf16[64,2,256]{2,1,0:T(2,128)(2,1)}), bf16[64,2,256]{2,1,0:T(2,128)(2,1)S(1)}, u32[]{:S(2)}, u32[]{:S(2)}) async-start(bf16[64,2,256]{2,1,0:T(2,128)(2,1)} %reshape.533), calls=%async_computation.1 | async-start | bytes 131072 | tf_op jit(solution)/shard_map/while/body/eval_jaxpr/all_to_all | solution.py:112
  296.6 14.6 %all-to-all-start = ((bf16[64,2,256]{2,1,0:T(2,128)(2,1)}), bf16[64,2,256]{2,1,0:T(2,128)(2,1)S(1)}, u32[]{:S(2)}, u32[]{:S(2)}) async-start(bf16[64,2,256]{2,1,0:T(2,128)(2,1)} %reshape.531), calls=%async_computation | async-start | bytes 131072 | tf_op jit(solution)/shard_map/while/body/eval_jaxpr/all_to_all | solution.py:81
  324.1 15.1 %all-to-all-start.1 = ((bf16[64,2,256]{2,1,0:T(2,128)(2,1)}), bf16[64,2,256]{2,1,0:T(2,128)(2,1)S(1)}, u32[]{:S(2)}, u32[]{:S(2)}) async-start(bf16[64,2,256]{2,1,0:T(2,128)(2,1)} %reshape.533), calls=%async_computation.1 | async-start | bytes 131072 | tf_op jit(solution)/shard_map/while/body/eval_jaxpr/all_to_all | solution.py:112
  341.4 14.6 %all-to-all-start = ((bf16[64,2,256]{2,1,0:T(2,128)(2,1)}), bf16[64,2,256]{2,1,0:T(2,128)(2,1)S(1)}, u32[]{:S(2)}, u32[]{:S(2)}) async-start(bf16[64,2,256]{2,1,0:T(2,128)(2,1)} %reshape.531), calls=%async_computation | async-start | bytes 131072 | tf_op jit(solution)/shard_map/while/body/eval_jaxpr/all_to_all | solution.py:81
  368.9 14.6 %all-to-all-start.1 = ((bf16[64,2,256]{2,1,0:T(2,128)(2,1)}), bf16[64,2,256]{2,1,0:T(2,128)(2,1)S(1)}, u32[]{:S(2)}, u32[]{:S(2)}) async-start(bf16[64,2,256]{2,1,0:T(2,128)(2,1)} %reshape.533), calls=%async_computation.1 | async-start | bytes 131072 | tf_op jit(solution)/shard_map/while/body/eval_jaxpr/all_to_all | solution.py:112
  385.7 14.6 %all-to-all-start = ((bf16[64,2,256]{2,1,0:T(2,128)(2,1)}), bf16[64,2,256]{2,1,0:T(2,128)(2,1)S(1)}, u32[]{:S(2)}, u32[]{:S(2)}) async-start(bf16[64,2,256]{2,1,0:T(2,128)(2,1)} %reshape.531), calls=%async_computation | async-start | bytes 131072 | tf_op jit(solution)/shard_map/while/body/eval_jaxpr/all_to_all | solution.py:81
  413.2 14.6 %all-to-all-start.1 = ((bf16[64,2,256]{2,1,0:T(2,128)(2,1)}), bf16[64,2,256]{2,1,0:T(2,128)(2,1)S(1)}, u32[]{:S(2)}, u32[]{:S(2)}) async-start(bf16[64,2,256]{2,1,0:T(2,128)(2,1)} %reshape.533), calls=%async_computation.1 | async-start | bytes 131072 | tf_op jit(solution)/shard_map/while/body/eval_jaxpr/all_to_all | solution.py:112
  430.1 14.6 %all-to-all-start = ((bf16[64,2,256]{2,1,0:T(2,128)(2,1)}), bf16[64,2,256]{2,1,0:T(2,128)(2,1)S(1)}, u32[]{:S(2)}, u32[]{:S(2)}) async-start(bf16[64,2,256]{2,1,0:T(2,128)(2,1)} %reshape.531), calls=%async_computation | async-start | bytes 131072 | tf_op jit(solution)/shard_map/while/body/eval_jaxpr/all_to_all | solution.py:81
  457.6 14.6 %all-to-all-start.1 = ((bf16[64,2,256]{2,1,0:T(2,128)(2,1)}), bf16[64,2,256]{2,1,0:T(2,128)(2,1)S(1)}, u32[]{:S(2)}, u32[]{:S(2)}) async-start(bf16[64,2,256]{2,1,0:T(2,128)(2,1)} %reshape.533), calls=%async_computation.1 | async-start | bytes 131072 | tf_op jit(solution)/shard_map/while/body/eval_jaxpr/all_to_all | solution.py:112
  474.4 14.6 %all-to-all-start = ((bf16[64,2,256]{2,1,0:T(2,128)(2,1)}), bf16[64,2,256]{2,1,0:T(2,128)(2,1)S(1)}, u32[]{:S(2)}, u32[]{:S(2)}) async-start(bf16[64,2,256]{2,1,0:T(2,128)(2,1)} %reshape.531), calls=%async_computation | async-start | bytes 131072 | tf_op jit(solution)/shard_map/while/body/eval_jaxpr/all_to_all | solution.py:81
  501.9 14.6 %all-to-all-start.1 = ((bf16[64,2,256]{2,1,0:T(2,128)(2,1)}), bf16[64,2,256]{2,1,0:T(2,128)(2,1)S(1)}, u32[]{:S(2)}, u32[]{:S(2)}) async-start(bf16[64,2,256]{2,1,0:T(2,128)(2,1)} %reshape.533), calls=%async_computation.1 | async-start | bytes 131072 | tf_op jit(solution)/shard_map/while/body/eval_jaxpr/all_to_all | solution.py:112
  518.7 14.6 %all-to-all-start = ((bf16[64,2,256]{2,1,0:T(2,128)(2,1)}), bf16[64,2,256]{2,1,0:T(2,128)(2,1)S(1)}, u32[]{:S(2)}, u32[]{:S(2)}) async-start(bf16[64,2,256]{2,1,0:T(2,128)(2,1)} %reshape.531), calls=%async_computation | async-start | bytes 131072 | tf_op jit(solution)/shard_map/while/body/eval_jaxpr/all_to_all | solution.py:81
  546.3 14.9 %all-to-all-start.1 = ((bf16[64,2,256]{2,1,0:T(2,128)(2,1)}), bf16[64,2,256]{2,1,0:T(2,128)(2,1)S(1)}, u32[]{:S(2)}, u32[]{:S(2)}) async-start(bf16[64,2,256]{2,1,0:T(2,128)(2,1)} %reshape.533), calls=%async_computation.1 | async-start | bytes 131072 | tf_op jit(solution)/shard_map/while/body/eval_jaxpr/all_to_all | solution.py:112
Sparse Core Ops, SparseCore 0:
  562.9 30.9 reduce-scatter.3
where the time goes:
time: 971 us; the launch traced here: 969 us
  blocking collectives  376 us (39%)
  waiting for transfers between devices  271 us (28%)
  matrix products  127 us (13%)
  starting transfers between devices  117 us (12%)
  local copies, waits for them, and re-layouts  56.9 us (6%)
  between operations  14.2 us (1%)
    psum x1, blocking collectives, body(): factor_grad = lax.psum(shared, 'cuts')  367 us
    all_to_all x12, waiting for transfers between devices, coil_step(): lax.all_to_all(zgrad, 'cuts', split_axis=2, concat_axis=4, tiled=True)  120 us
    all_to_all x12, waiting for transfers between devices, coil_step(): lax.all_to_all(hybrid, 'cuts', split_axis=4, concat_axis=2, tiled=True)  120 us
    all_to_all x12, starting transfers between devices, coil_step(): lax.all_to_all(hybrid, 'cuts', split_axis=4, concat_axis=2, tiled=True)  61.1 us
    all_to_all x12, starting transfers between devices, coil_step(): lax.all_to_all(zgrad, 'cuts', split_axis=2, concat_axis=4, tiled=True)  55.6 us
    unnamed x2, waiting for transfers between devices  30.4 us
    dot_general x12, matrix products, coil_step(): pred_re = jnp.einsum('tsc,xtc->tsx', onehot32, mixed_re, precision=HIGH)  25 us
    dot_general x12, matrix products, coil_step(): pred_im = jnp.einsum('tsc,xtc->tsx', onehot32, mixed_im, precision=HIGH)  25 us
  transfers between devices with their start and end apart: 25, of which 25 were waited for; matrix products, arithmetic and copies ran while one was open for 0% of the time, Pallas kernels for 0%

commit v1 on v0

v1 whole, which is shorter than its diff:
```python
import math

import jax
import jax.numpy as jnp
import numpy as np
from jax import lax
from jax.sharding import PartitionSpec as P

BF = jnp.bfloat16
F32 = jnp.float32


def dft_np(size):
    index = np.arange(size)
    angle = (index[:, None] * index[None, :] % size) * (2.0 * math.pi / size)
    return np.cos(angle) / math.sqrt(size), -np.sin(angle) / math.sqrt(size)


def dot(spec, a, b):
    return jnp.einsum(spec, a, b, preferred_element_type=F32)


def body(basis, coil_maps, factors, lines, kdata):
    n_cuts = lax.axis_size("cuts")
    cuts = lax.axis_index("cuts")
    rank, slab, width = basis.shape[1], basis.shape[2], basis.shape[4]
    coils = coil_maps.shape[1]
    depth = slab * n_cuts
    rows = width // n_cuts
    lpd = lines.shape[1]
    scale = 1.0 / math.sqrt(coils * lpd * n_cuts * basis.shape[3] * lax.axis_size("frame"))
    cy, sy = dft_np(width)
    perm = (np.arange(rows)[:, None] + rows * np.arange(n_cuts)[None, :]).reshape(-1)
    c, s = cy[:, perm], sy[:, perm]
    table = jnp.asarray(np.block([[c, s], [-s, c]]), BF)

    v = lax.all_gather(factors, "frame", axis=2, tiled=True)
    frames = v.shape[2]
    every = lax.all_gather(lines, "cuts", axis=0)
    kz = every % depth
    row = every // depth
    b = basis[:, :, :, 0].astype(F32)
    m = coil_maps[:, :, :, 0].astype(F32)
    image = jnp.stack(
        [
            m[0][:, :, None] * b[0].transpose(1, 0, 2)[None] - m[1][:, :, None] * b[1].transpose(1, 0, 2)[None],
            m[0][:, :, None] * b[1].transpose(1, 0, 2)[None] + m[1][:, :, None] * b[0].transpose(1, 0, 2)[None],
        ],
        axis=3,
    ).astype(BF)
    image = image.reshape(coils * slab * rank, 2 * width)
    hybrid = jnp.dot(image, table, preferred_element_type=F32).astype(BF)
    hybrid = hybrid.reshape(coils, slab, rank, 2, width)
    vr, vi = v[0], v[1]
    mixer = jnp.stack([jnp.stack([vr, -vi]), jnp.stack([vi, vr])])
    mixed = dot("czlpw,qplt->czqtw", hybrid, mixer).reshape(coils, slab, 2, frames, rows, n_cuts)
    zpos = cuts * slab + jnp.arange(slab)
    angle = (kz[None] * zpos[:, None, None, None] % depth).astype(F32) * (2.0 * math.pi / depth)
    pr = (jnp.cos(angle) / math.sqrt(depth)).astype(BF).astype(F32)
    pi = (-jnp.sin(angle) / math.sqrt(depth)).astype(BF).astype(F32)
    pr = pr.transpose(0, 3, 2, 1)
    pi = pi.transpose(0, 3, 2, 1)
    row = row.transpose(2, 1, 0)
    parts = []
    for sample in range(lpd):
        r = row[sample]
        sel = sum(
            jnp.where(r == k, mixed[:, :, :, :, k], 0.0) for k in range(rows)
        )
        re = jnp.sum(sel[:, :, 0] * pr[None, :, sample] - sel[:, :, 1] * pi[None, :, sample], 1)
        im = jnp.sum(sel[:, :, 0] * pi[None, :, sample] + sel[:, :, 1] * pr[None, :, sample], 1)
        parts.append(jnp.stack([re, im]))
    part = jnp.stack(parts)
    part = part.transpose(4, 2, 1, 0, 3).reshape(n_cuts, -1).astype(BF)
    pred = lax.psum_scatter(part, "cuts", scatter_dimension=0, tiled=True)
    kd = kdata[..., 0].transpose(3, 0, 2, 1).reshape(1, -1)
    resid = (pred.astype(F32) - kd.astype(F32)).astype(BF)
    whole = lax.all_gather(resid, "cuts", axis=0, tiled=True)
    whole = whole.reshape(n_cuts, coils, 2, lpd, frames).transpose(3, 2, 1, 4, 0).astype(F32)
    spread = 0.0
    for sample in range(lpd):
        x, y = whole[sample, 0][:, None], whole[sample, 1][:, None]
        re = x * pr[None, :, sample] + y * pi[None, :, sample]
        im = y * pr[None, :, sample] - x * pi[None, :, sample]
        e = jnp.stack([re, im], 2)
        r = row[sample]
        spread = spread + jnp.stack([jnp.where(r == k, e, 0.0) for k in range(rows)], 4)
    spread = spread.astype(BF).reshape(coils, slab, 2, frames, width)
    outer = dot("czlpw,czqtw->plqt", hybrid, spread)
    gv = jnp.stack([outer[0, :, 0] + outer[1, :, 1], outer[0, :, 1] - outer[1, :, 0]])
    unmix = jnp.stack([jnp.stack([vr, vi]), jnp.stack([-vi, vr])])
    zgrad = dot("czptw,qplt->czlqw", spread, unmix).astype(BF)
    zgrad = zgrad.reshape(coils * slab * rank, 2 * width)
    back = lax.dot_general(zgrad, table, (((1,), (1,)), ((), ())), preferred_element_type=F32)
    back = back.reshape(coils, slab, rank, 2, width)
    gr = jnp.sum(m[0][:, :, None] * back[:, :, :, 0] + m[1][:, :, None] * back[:, :, :, 1], 0)
    gi = jnp.sum(m[0][:, :, None] * back[:, :, :, 1] - m[1][:, :, None] * back[:, :, :, 0], 0)
    grad = jnp.stack([gr, gi]).transpose(0, 2, 1, 3)[:, :, :, None]
    shared = lax.psum_scatter(gv * scale, "frame", scatter_dimension=2, tiled=True)
    return grad, lax.psum(shared, "cuts")


def solution(mesh):
    placed = (
        P(None, None, "cuts", "frame", None),
        P(None, None, "cuts", "frame", None),
        P(None, None, "frame"),
        P(None, "cuts"),
        P(None, None, "cuts", None, "frame"),
    )
    return jax.shard_map(
        body,
        mesh=mesh,
        in_specs=placed,
        out_specs=(P(None, None, "cuts", "frame", None), P(None, None, "frame")),
        check_vma=False,
    )
```

time: 971 us -> 1550 us (1.60)
  waiting for transfers between devices: 271 us -> 683 us
  blocking collectives: 376 us -> 765 us
  matrix products: 127 us -> 5.9 us
  starting transfers between devices: 117 us -> 0.04 us
  other arithmetic: 4.58 us -> 46.4 us
  local copies, waits for them, and re-layouts: 56.9 us -> 35 us
    unnamed x2, waiting for transfers between devices: 30.4 us -> 683 us
    all_gather x1 -> x3, blocking collectives: 9.27 us -> 385 us  [the longest x1 189 us: body(): whole = lax.all_gather(resid, 'cuts', axis=0, tiled=True)]
    all_to_all x24 -> x0, waiting for transfers between devices: 240 us -> none  [the longest x12 120 us: coil_step(): lax.all_to_all(zgrad, 'cuts', split_axis=2, concat_axis=4, tiled=True)]
    dot_general x228 -> x5, matrix products: 127 us -> 5.9 us  [the longest x3 4.73 us: dot(): return jnp.einsum(spec, a, b, preferred_element_type=F32)]
    all_to_all x24 -> x0, starting transfers between devices: 117 us -> none  [the longest x12 61.1 us: coil_step(): lax.all_to_all(hybrid, 'cuts', split_axis=4, concat_axis=2, tiled=True)]
    while x48 -> x0, local copies, waits for them, and re-layouts: 24.3 us -> none
    select_n x0 -> x3, other arithmetic: none -> 19.3 us  [body(): jnp.where(r == k, e, 0.0)]
    unnamed x0 -> x1, blocking collectives: none -> 18.8 us
  transfers between devices with their start and end apart: 25 -> 1, of which waited for: 25 -> 1; matrix products, arithmetic and copies ran while one was open for 0% -> 0% of each run, Pallas kernels for 0% -> 0%
where the time goes in v1:
time: 1550 us
  blocking collectives  765 us (49%)
  waiting for transfers between devices  683 us (44%)
  other arithmetic  46.4 us (3%)
  local copies, waits for them, and re-layouts  35 us (2%)
  between operations  15.6 us (1%)
    unnamed x2, waiting for transfers between devices  683 us
    psum x1, blocking collectives, body(): return (grad, lax.psum(shared, 'cuts'))  362 us
    all_gather x1, blocking collectives, body(): whole = lax.all_gather(resid, 'cuts', axis=0, tiled=True)  189 us
    all_gather x1, blocking collectives, body(): every = lax.all_gather(lines, 'cuts', axis=0)  187 us
  transfers between devices with their start and end apart: 1, of which 1 were waited for; matrix products, arithmetic and copies ran while one was open for 0% of the time, Pallas kernels for 0%

profile of v1, /device:TPU:0, one launch (start us, length us, event | category | flops | bytes accessed | tf_op | source)
XLA Modules:
  0.0 1550.7 jit_solution(7144732709453119394)
XLA Ops:
  7.2 0.7 copy.101
  7.9 9.1 all_gather.12
  17.1 0.8 convert_element_type.92
  17.9 186.8 %all-gather.1 = s32[64,64,2]{1,2,0:T(2,128)S(1)} all-gather(s32[1,64,2]{1,2,0:T(2,128)} %bitcast.244), channel_id=2, replica_groups=mesh['cuts'=64,'frame'=4] {'cuts'}, dimensions={0}, use_global_device_ids=true | all-gather | bytes 33280 | tf_op jit(solution)/shard_map/all_gather | solution.py:39
  205.0 0.9 convert_element_type.93
  206.7 1.6 subtract_convert_fusion
  208.3 1.8 pad_maximum_fusion.2
  210.9 1.1 reshape.326
  212.6 1.7 convolution_bitcast_fusion
  214.3 4.4 reshape.327
  218.7 12.0 fusion.43
  230.8 0.8 select_add_fusion.1
  232.6 0.8 copy.115
  233.4 1.3 convert_element_type.102
  234.8 0.7 dynamic-slice.2
  236.8 682.6 %all-reduce.4.cloned.1.call-done = bf16[64,3072]{1,0:T(8,128)(2,1)} async-done(((bf16[64,3072]{1,0:T(8,128)(2,1)}), bf16[64,3072]{1,0:T(8,128)(2,1)}) %all-reduce.4.cloned.1.call-update) | async-done | bytes 393232
  919.5 1.4 fusion.40
  920.8 188.8 %all-gather.2 = bf16[64,1,3072]{2,1,0:T(2,128)(2,1)S(1)} all-gather(bf16[1,1,3072]{2,1,0:T(2,128)(2,1)S(1)} %fusion.40), channel_id=1, replica_groups=mesh['cuts'=64,'frame'=4] {'cuts'}, dimensions={0}, use_global_device_ids=true | all-gather | bytes 399360 | tf_op jit(solution)/shard_map/all_gather | solution.py:78
  1109.6 2.2 convert_reduce_fusion
  1111.8 1.1 reshape.329
  1113.0 1.2 fusion.44
  1116.5 3.5 broadcast_select_fusion.3
  1120.1 3.6 broadcast_select_fusion.7
  1123.7 12.3 broadcast_select_fusion.2
  1136.0 14.7 fusion
  1150.7 3.0 reshape.347
  1153.7 3.0 convert_element_type.113
  1156.6 2.6 fusion.11
  1159.7 0.8 copy.124
  1161.1 18.8 %all-reduce.1 = f32[2,32,64]{1,0,2:T(2,128)S(1)} all-reduce(f32[2,32,64]{1,0,2:T(2,128)S(1)} %copy.129), channel_id=4, replica_groups=mesh['cuts'=64,'frame'=4] {'frame'}, use_global_device_ids=true, to_apply=%region_7.8.clone | all-reduce | flops 4096 | bytes 32768
  1180.0 361.6 %psum.7 = f32[2,32,16]{1,0,2:T(2,128)S(1)} all-reduce(f32[2,32,16]{1,0,2:T(2,128)S(1)} %constant_dynamic-slice_fusion), channel_id=1, replica_groups=mesh['cuts'=64,'frame'=4] {'cuts'}, use_global_device_ids=true, to_apply=%region_8.9 | all-reduce | flops 1024 | bytes 8192 | tf_op jit(solution)/shard_map/psum | solution.py:100
  1543.1 0.8 copy.130
  (114 shorter events, 8.7 us)
Async XLA Ops:
  7.2 912.3 %all-reduce.4.cloned.1.call-start = ((), (), s32[]{:S(2)}) async-start(), calls=%async_computation | async-start | bytes 786432
  17.9 190.4 %copy-start.10 = (f32[12,2,256]{2,1,0:T(2,128)}, f32[12,2,256]{2,1,0:T(2,128)S(1)}, u32[]{:S(2)}) copy-start(f32[12,2,256]{2,1,0:T(2,128)S(1)} %get-tuple-element.60) | copy-start | bytes 73732
  17.9 190.4 %copy-start.12 = (f32[12,2,256]{2,1,0:T(2,128)}, f32[12,2,256]{2,1,0:T(2,128)S(1)}, u32[]{:S(2)}) copy-start(f32[12,2,256]{2,1,0:T(2,128)S(1)} %get-tuple-element.61) | copy-start | bytes 73732
  205.0 25.8 %copy-start.14 = (pred[64,64]{1,0:T(8,128)(4,1)}, pred[64,64]{1,0:T(8,128)(4,1)S(1)}, u32[]{:S(2)}) copy-start(pred[64,64]{1,0:T(8,128)(4,1)S(1)} %get-tuple-element.50) | copy-start | bytes 12292
  205.0 25.8 %copy-start.16 = (pred[64,64]{1,0:T(8,128)(4,1)}, pred[64,64]{1,0:T(8,128)(4,1)S(1)}, u32[]{:S(2)}) copy-start(pred[64,64]{1,0:T(8,128)(4,1)S(1)} %get-tuple-element.51) | copy-start | bytes 12292
  205.0 25.8 %copy-start.18 = (pred[64,64]{1,0:T(8,128)(4,1)}, pred[64,64]{1,0:T(8,128)(4,1)S(1)}, u32[]{:S(2)}) copy-start(pred[64,64]{1,0:T(8,128)(4,1)S(1)} %get-tuple-element.52) | copy-start | bytes 12292
  205.0 25.8 %copy-start.20 = (pred[64,64]{1,0:T(8,128)(4,1)}, pred[64,64]{1,0:T(8,128)(4,1)S(1)}, u32[]{:S(2)}) copy-start(pred[64,64]{1,0:T(8,128)(4,1)S(1)} %get-tuple-element.53) | copy-start | bytes 12292
  205.0 25.8 %copy-start.22 = (pred[64,64]{1,0:T(8,128)(4,1)}, pred[64,64]{1,0:T(8,128)(4,1)S(1)}, u32[]{:S(2)}) copy-start(pred[64,64]{1,0:T(8,128)(4,1)S(1)} %get-tuple-element.54) | copy-start | bytes 12292
  205.0 25.8 %copy-start.24 = (pred[64,64]{1,0:T(8,128)(4,1)}, pred[64,64]{1,0:T(8,128)(4,1)S(1)}, u32[]{:S(2)}) copy-start(pred[64,64]{1,0:T(8,128)(4,1)S(1)} %get-tuple-element.55) | copy-start | bytes 12292
  205.0 25.8 %copy-start.26 = (pred[64,64]{1,0:T(8,128)(4,1)}, pred[64,64]{1,0:T(8,128)(4,1)S(1)}, u32[]{:S(2)}) copy-start(pred[64,64]{1,0:T(8,128)(4,1)S(1)} %get-tuple-element.57) | copy-start | bytes 12292
  205.0 25.8 %copy-start.28 = (pred[64,64]{1,0:T(8,128)(4,1)}, pred[64,64]{1,0:T(8,128)(4,1)S(1)}, u32[]{:S(2)}) copy-start(pred[64,64]{1,0:T(8,128)(4,1)S(1)} %get-tuple-element.56) | copy-start | bytes 12292
  206.6 25.0 %copy-start.5 = (f32[2,64,64]{2,1,0:T(8,128)}, f32[2,64,64]{2,1,0:T(8,128)S(1)}, u32[]{:S(2)}) copy-start(f32[2,64,64]{2,1,0:T(8,128)S(1)} %get-tuple-element.42) | copy-start | bytes 98308
  206.6 25.4 %copy-start.1 = (f32[2,64,64]{2,1,0:T(8,128)}, f32[2,64,64]{2,1,0:T(8,128)S(1)}, u32[]{:S(2)}) copy-start(f32[2,64,64]{2,1,0:T(8,128)S(1)} %get-tuple-element.43) | copy-start | bytes 98308
  206.6 25.0 %copy-start.7 = (f32[2,64,64]{2,1,0:T(8,128)}, f32[2,64,64]{2,1,0:T(8,128)S(1)}, u32[]{:S(2)}) copy-start(f32[2,64,64]{2,1,0:T(8,128)S(1)} %get-tuple-element.45) | copy-start | bytes 98308
  206.7 25.4 %copy-start.3 = (f32[2,64,64]{2,1,0:T(8,128)}, f32[2,64,64]{2,1,0:T(8,128)S(1)}, u32[]{:S(2)}) copy-start(f32[2,64,64]{2,1,0:T(8,128)S(1)} %get-tuple-element.44) | copy-start | bytes 98308
  208.3 2.0 copy-start.32
  232.6 2.2 copy-start.34
  232.6 2.8 copy-start.33
  232.6 3.4 copy-start.31
  1114.2 1.3 copy-start.6
  1116.5 3.5 copy-start.27
  1120.0 3.6 copy-start.15
  1120.0 3.6 copy-start.17
  1120.0 3.6 copy-start.19
  1120.1 3.6 copy-start.21
  1120.1 3.6 copy-start.23
  1120.1 3.6 copy-start.25
  1156.6 2.6 copy-start
  1156.6 2.6 copy-start.30
  1159.7 382.5 %copy-start.9 = (bf16[2,256,512,1,1]{2,1,0,4,3:T(8,128)(2,1)S(1)}, bf16[2,256,512,1,1]{2,1,0,4,3:T(8,128)(2,1)}, u32[]{:S(2)}) copy-start(bf16[2,256,512,1,1]{2,1,0,4,3:T(8,128)(2,1)} %constant.75) | copy-start | bytes 1572868
  1161.1 381.7 %copy-start.11 = (f32[12,2,256]{2,1,0:T(2,128)S(1)}, f32[12,2,256]{2,1,0:T(2,128)}, u32[]{:S(2)}) copy-start(f32[12,2,256]{2,1,0:T(2,128)} %copy-done.10) | copy-start | bytes 73732
  1161.1 381.7 %copy-start.13 = (f32[12,2,256]{2,1,0:T(2,128)S(1)}, f32[12,2,256]{2,1,0:T(2,128)}, u32[]{:S(2)}) copy-start(f32[12,2,256]{2,1,0:T(2,128)} %copy-done.12) | copy-start | bytes 73732
  (4 other events, 3.8 us)
Sparse Core Ops, SparseCore 0:
  234.9 684.5 all-reduce.3

commit v2 on v1

v2 whole, which is shorter than its diff:
```python
import functools
import math

import jax
import jax.numpy as jnp
import numpy as np
from jax import lax
from jax.experimental import pallas as pl
from jax.experimental.pallas import tpu as pltpu
from jax.sharding import PartitionSpec as P

BF = jnp.bfloat16
F32 = jnp.float32
I32 = jnp.int32
GROUP = 4
ROWS = 4


def real_table(size, blocks):
    index = np.arange(size)
    angle = (index[:, None] * index[None, :] % size) * (2.0 * math.pi / size)
    cosine, sine = np.cos(angle) / math.sqrt(size), np.sin(angle) / math.sqrt(size)
    order = (np.arange(ROWS)[:, None] + ROWS * np.arange(blocks)[None, :]).reshape(-1)
    c, s = cosine[order], sine[order]
    return np.block([[c, s], [-s, c]])


def nn(a, b):
    return jnp.dot(a, b, preferred_element_type=F32)


def nt(a, b):
    return lax.dot_general(a, b, (((1,), (1,)), ((), ())), preferred_element_type=F32)


def iota(shape, axis):
    return lax.broadcasted_iota(I32, shape, axis)


def kernel(
    dims,
    scale,
    b_ref,
    m_ref,
    v_ref,
    l_ref,
    d_ref,
    t_ref,
    grad_ref,
    fg_ref,
    img,
    ht,
    hn,
    pb,
    vbt,
    vc,
    ph,
    rowid,
    perm,
    permt,
    sx,
    xr,
    sy,
    yr,
    sz,
    zr,
    ra,
    lg,
    vg,
    kg,
    kd,
    zg,
    gv,
    gs,
    gr,
    send,
    rx,
    ry,
    rz,
    ray,
    rax,
    rl,
    rv,
    rk,
    rg,
):
    na, nb, nc, nf, chunks = dims
    slab, parts, rank, width = b_ref.shape
    frames = 64
    blocks = na * nb * nc
    depth = slab * blocks
    me = lax.axis_index("cuts")
    fr = lax.axis_index("frame")
    ia, ib, ic = me // (nb * nc), (me // nc) % nb, me % nc
    lane = 2 * frames
    sl = slab * rank

    def peer_a(j):
        return {"cuts": lax.rem(ia + j, na) * (nb * nc) + ib * nc + ic}

    def peer_b(j):
        return {"cuts": ia * (nb * nc) + lax.rem(ib + j, nb) * nc + ic}

    def peer_c(j):
        return {"cuts": ia * (nb * nc) + ib * nc + lax.rem(ic + j, nc)}

    def peer_f(j):
        return {"frame": lax.rem(fr + j, nf)}

    def remote(src, dst, s, r, who):
        return pltpu.make_async_remote_copy(
            src_ref=src,
            dst_ref=dst,
            send_sem=s,
            recv_sem=r,
            device_id=who,
            device_id_type=pl.DeviceIdType.MESH,
        )

    everyone = (
        [peer_a(j) for j in range(1, na)]
        + [peer_b(j) for j in range(1, nb)]
        + [peer_c(j) for j in range(1, nc)]
        + [peer_f(j) for j in range(1, nf)]
    )
    barrier = pltpu.get_barrier_semaphore()
    for who in everyone:
        pl.semaphore_signal(barrier, inc=1, device_id=who, device_id_type=pl.DeviceIdType.MESH)

    lg[pl.ds(me, 1)] = l_ref[...][None]
    vg[pl.ds(fr, 1)] = v_ref[...][None]
    kg[pl.ds(ic, 1)] = d_ref[...][None]

    n_rows = GROUP * blocks
    out_row = iota((n_rows, n_rows), 0)
    in_row = iota((n_rows, n_rows), 1)

    def spot(r):
        return (r // nc) % GROUP * blocks + r // (nc * GROUP) * nc + r % nc

    perm[...] = (spot(out_row) == in_row).astype(F32).astype(BF)
    permt[...] = (spot(in_row) == out_row).astype(F32).astype(BF)

    def forward(k, carry):
        for c4 in range(GROUP):
            for z in range(slab):
                base = ((k * GROUP + c4) * slab + z) * 2
                mr, mi = m_ref[base], m_ref[base + 1]
                br, bi = b_ref[z, 0].astype(F32), b_ref[z, 1].astype(F32)
                at = (c4 * slab + z) * rank
                img[k, at : at + rank, 0:width] = (mr * br - mi * bi).astype(BF)
                img[k, at : at + rank, width : 2 * width] = (mr * bi + mi * br).astype(BF)
        ht[k] = nt(t_ref[...], img[k]).astype(BF)
        return carry

    lax.fori_loop(0, chunks, forward, 0)

    pl.semaphore_wait(barrier, len(everyone))

    vcopies = [
        remote(vg.at[fr], vg.at[fr], send.at[0, j], rv.at[j], peer_f(j)) for j in range(1, nf)
    ]
    lc = [
        remote(lg.at[pl.ds(me, 1)], lg.at[pl.ds(me, 1)], send.at[1, j], rl.at[0, j], peer_c(j))
        for j in range(1, nc)
    ]
    kcopies = [
        remote(kg.at[ic], kg.at[ic], send.at[2, j], rk.at[j], peer_c(j)) for j in range(1, nc)
    ]
    for copy in lc + vcopies + kcopies:
        copy.start()
    for copy in lc:
        copy.wait()
    low = (ia * nb + ib) * nc
    lb = [
        remote(lg.at[pl.ds(low, nc)], lg.at[pl.ds(low, nc)], send.at[3, j], rl.at[1, j], peer_b(j))
        for j in range(1, nb)
    ]
    for copy in lb:
        copy.start()
    for copy in vcopies:
        copy.wait()

    vt = [vg[:, p].reshape(frames, rank) for p in range(2)]
    rep = (iota((rank, 4 * rank), 0) == iota((rank, 4 * rank), 1) % rank).astype(F32).astype(BF)
    wide = [nn(vt[p], rep) for p in range(2)]
    block_of = iota((frames, 4 * rank), 1) // rank
    for blk in range(4):
        r_ = jnp.where(block_of == blk, wide[0], 0.0).astype(BF)
        i_ = jnp.where(block_of == blk, wide[1], 0.0).astype(BF)
        at = blk * frames
        vbt[at : at + frames, 0 : 4 * rank] = r_
        vbt[at : at + frames, 4 * rank : 8 * rank] = -i_
        at = (4 + blk) * frames
        vbt[at : at + frames, 0 : 4 * rank] = i_
        vbt[at : at + frames, 4 * rank : 8 * rank] = r_
    rep2 = (iota((sl, rank), 0) % rank == iota((sl, rank), 1)).astype(F32).astype(BF)
    same = iota((sl, lane), 0) // rank == iota((sl, lane), 1) // frames
    tall = [nt(rep2, jnp.concatenate([vt[p], vt[p]], 0)) for p in range(2)]
    r_ = jnp.where(same, tall[0], 0.0).astype(BF)
    i_ = jnp.where(same, tall[1], 0.0).astype(BF)
    vc[0:sl, 0:lane] = r_
    vc[0:sl, lane : 2 * lane] = i_
    vc[sl : 2 * sl, 0:lane] = -i_
    vc[sl : 2 * sl, lane : 2 * lane] = r_

    for copy in lb:
        copy.wait()
    low = ia * nb * nc
    la = [
        remote(
            lg.at[pl.ds(low, nb * nc)],
            lg.at[pl.ds(low, nb * nc)],
            send.at[4, j],
            rl.at[2, j],
            peer_a(j),
        )
        for j in range(1, na)
    ]
    for copy in la:
        copy.start()

    def again(k, carry):
        full = nt(img[k], t_ref[...]).astype(BF)
        for c4 in range(GROUP):
            hn[k, c4, 0:sl, :] = full[c4 * sl : (c4 + 1) * sl, 0:width]
            hn[k, c4, sl : 2 * sl, :] = full[c4 * sl : (c4 + 1) * sl, width : 2 * width]
        return carry

    lax.fori_loop(0, chunks, again, 0)

    for copy in kcopies:
        copy.wait()
    kall = kg[...].reshape(nc * 16, 2 * lane)
    krow = iota((chunks * GROUP * nc, nc * 16), 0)
    kcol = iota((chunks * GROUP * nc, nc * 16), 1)
    pick = (krow % nc * 16 + krow // nc == kcol).astype(F32).astype(BF)
    kd[...] = nn(pick, kall).reshape(chunks, GROUP * nc, 2 * lane)

    for copy in la:
        copy.wait()

    lo = iota((blocks, lane), 1) < frames
    every = lg[...].reshape(blocks, lane)
    turned = pltpu.roll(every, frames, 1)
    zpos = me * slab + iota((blocks, lane), 1) // frames
    norm = 1.0 / math.sqrt(depth)
    for s in range(2):
        mine = jnp.where(lo, every, turned) if s == 0 else jnp.where(lo, turned, every)
        kz = lax.rem(mine, depth)
        rowid[s] = lax.div(mine, depth)
        angle = lax.rem(kz * zpos, depth).astype(F32) * (2.0 * math.pi / depth)
        ph[s, 0] = (jnp.cos(angle) * norm).astype(BF).astype(F32)
        ph[s, 1] = (jnp.sin(angle) * -norm).astype(BF).astype(F32)

    def parts_of(k, carry):
        for pair in range(GROUP // 2):
            at = pair * 2 * sl
            lhs = jnp.concatenate(
                [ht[k, 0:width, at : at + 2 * sl], ht[k, width : 2 * width, at : at + 2 * sl]], 1
            )
            mixed = nt(lhs, vbt[...])
            for c2 in range(2):
                re0, im0 = c2 * lane, (2 + c2) * lane
                got = []
                for s in range(2):
                    rs = rowid[s]
                    mr = mixed[0:blocks, re0 : re0 + lane]
                    mi = mixed[0:blocks, im0 : im0 + lane]
                    for r in range(1, ROWS):
                        here = rs == r
                        mr = jnp.where(here, mixed[r * blocks : (r + 1) * blocks, re0 : re0 + lane], mr)
                        mi = jnp.where(here, mixed[r * blocks : (r + 1) * blocks, im0 : im0 + lane], mi)
                    pr, pi = ph[s, 0], ph[s, 1]
                    got.append((pr * mr - pi * mi, pr * mi + pi * mr))
                row = (pair * 2 + c2) * blocks
                for q in range(2):
                    keep = jnp.where(lo, got[0][q], got[1][q])
                    fold = jnp.where(lo, got[1][q], got[0][q])
                    total = keep + pltpu.roll(fold, frames, 1)
                    pb[row : row + blocks, q * lane : (q + 1) * lane] = total.astype(BF)
        part = nn(perm[...], pb[...]).astype(BF)
        sx[k] = part.reshape(na, nb, GROUP * nc, 2 * lane)
        for j in range(1, na):
            to_a(k, j).start()
        return carry

    def to_a(k, j):
        return remote(
            sx.at[k, lax.rem(ia + j, na)], xr.at[k, j], send.at[5 + k, j], rx.at[k, j], peer_a(j)
        )

    def to_b(k, j):
        return remote(
            sy.at[k, lax.rem(ib + j, nb)], yr.at[k, j], send.at[8 + k, j], ry.at[k, j], peer_b(j)
        )

    def to_c(k, j):
        return remote(sz.at[k], zr.at[k, j], send.at[11 + k, j], rz.at[k, j], peer_c(j))

    def back_b(k, j):
        return remote(
            ra.at[k, ia, ib], ra.at[k, ia, ib], send.at[14 + k, j], ray.at[k, j], peer_b(j)
        )

    def back_a(k, j):
        return remote(ra.at[k, ia], ra.at[k, ia], send.at[17 + k, j], rax.at[k, j], peer_a(j))

    lax.fori_loop(0, chunks, parts_of, 0)

    for k in range(chunks):
        total = sx[k, ia].astype(F32)
        for j in range(1, na):
            to_a(k, j).wait()
            total = total + xr[k, j].astype(F32)
        sy[k] = total.astype(BF)
        for j in range(1, nb):
            to_b(k, j).start()
    for k in range(chunks):
        total = sy[k, ib].astype(F32)
        for j in range(1, nb):
            to_b(k, j).wait()
            total = total + yr[k, j].astype(F32)
        sz[k] = total.astype(BF)
        for j in range(1, nc):
            to_c(k, j).start()
    for k in range(chunks):
        total = sz[k].astype(F32)
        for j in range(1, nc):
            to_c(k, j).wait()
            total = total + zr[k, j].astype(F32)
        ra[k, ia, ib] = (total - kd[k]).astype(BF)
        for j in range(1, nb):
            back_b(k, j).start()
    for k in range(chunks):
        for j in range(1, nb):
            back_b(k, j).wait()
        for j in range(1, na):
            back_a(k, j).start()

    grad_ref[...] = jnp.zeros_like(grad_ref)
    gv[...] = jnp.zeros_like(gv)

    def backward(k, carry):
        for j in range(1, na):
            back_a(k, j).wait()
        resid = nn(permt[...], ra[k].reshape(n_rows, 2 * lane))
        for c4 in range(GROUP):
            here = [resid[c4 * blocks : (c4 + 1) * blocks, q * lane : (q + 1) * lane] for q in range(2)]
            flip = [pltpu.roll(x, frames, 1) for x in here]
            terms = []
            for s in range(2):
                xr_, xi_ = [
                    jnp.where(lo, a, b) if s == 0 else jnp.where(lo, b, a) for a, b in zip(here, flip)
                ]
                pr, pi = ph[s, 0], ph[s, 1]
                terms.append((xr_ * pr + xi_ * pi, xi_ * pr - xr_ * pi))
            spread = []
            for r in range(ROWS):
                m0, m1 = rowid[0] == r, rowid[1] == r
                spread.append(
                    jnp.concatenate(
                        [
                            (
                                jnp.where(m0, terms[0][q], 0.0) + jnp.where(m1, terms[1][q], 0.0)
                            ).astype(BF)
                            for q in range(2)
                        ],
                        1,
                    )
                )
            e = jnp.concatenate(spread, 0)
            zc = nt(vc[...], e).astype(BF)
            zg[c4 * sl : (c4 + 1) * sl, 0:width] = zc[0:sl]
            zg[c4 * sl : (c4 + 1) * sl, width : 2 * width] = zc[sl : 2 * sl]
            gv[...] += nn(hn[k, c4], e)
        back = nn(zg[...], t_ref[...])
        for z in range(slab):
            re, im = grad_ref[0, z], grad_ref[1, z]
            for c4 in range(GROUP):
                base = ((k * GROUP + c4) * slab + z) * 2
                mr, mi = m_ref[base], m_ref[base + 1]
                at = (c4 * slab + z) * rank
                br = back[at : at + rank, 0:width]
                bi = back[at : at + rank, width : 2 * width]
                re = re + mr * br + mi * bi
                im = im + mr * bi - mi * br
            grad_ref[0, z], grad_ref[1, z] = re, im
        return carry

    lax.fori_loop(0, chunks, backward, 0)

    g = gv[...]
    own = {}
    for p in range(2):
        for q in range(2):
            first = g[p * sl : p * sl + rank, q * lane : (q + 1) * lane]
            second = g[p * sl + rank : (p + 1) * sl, q * lane : (q + 1) * lane]
            own[p, q] = first + pltpu.roll(second, frames, 1)
    gre = (own[0, 0] + own[1, 1]) * scale
    gim = (own[0, 1] - own[1, 0]) * scale
    turned = jnp.transpose(jnp.concatenate([gre, gim, gre, gim], 0))
    span = frames // nf
    gs[0:nf] = turned[0:frames].reshape(nf, span, 4 * rank)

    copies = [
        remote(gs.at[lax.rem(fr + j, nf)], gr.at[0, j], send.at[20, j], rg.at[0, j], peer_f(j))
        for j in range(1, nf)
    ]
    for copy in copies:
        copy.start()
    total = gs[fr]
    for j, copy in enumerate(copies):
        copy.wait()
        total = total + gr[0, j + 1]
    for level, (count, peer) in enumerate(((nc, peer_c), (nb, peer_b), (na, peer_a))):
        gs[nf + level] = total
        copies = [
            remote(
                gs.at[nf + level],
                gr.at[1 + level, j],
                send.at[21 + level, j],
                rg.at[1 + level, j],
                peer(j),
            )
            for j in range(1, count)
        ]
        for copy in copies:
            copy.start()
        for j, copy in enumerate(copies):
            copy.wait()
            total = total + gr[1 + level, j + 1]
    fg_ref[...] = total


SHAPES = {64: (4, 4, 4), 8: (2, 2, 2)}


def body(basis, coil_maps, factors, lines, kdata):
    n_cuts = lax.axis_size("cuts")
    nf = lax.axis_size("frame")
    na, nb, nc = SHAPES[n_cuts]
    rank, slab, width = basis.shape[1], basis.shape[2], basis.shape[4]
    coils = coil_maps.shape[1]
    chunks = coils // GROUP
    span = factors.shape[2]
    lpd = lines.shape[1]
    frames = span * nf
    lane = 2 * frames
    sl = slab * rank
    blocks = n_cuts
    n_rows = GROUP * blocks
    scale = 1.0 / math.sqrt(coils * lpd * n_cuts * basis.shape[3] * nf)
    table = jnp.asarray(real_table(width, n_cuts), BF)
    b = basis[:, :, :, 0].transpose(2, 0, 1, 3)
    m = coil_maps[:, :, :, 0].transpose(1, 2, 0, 3).reshape(coils * slab * 2, 1, width).astype(F32)
    v = factors.transpose(0, 2, 1)
    l = lines.T.reshape(1, lane)
    d = jnp.pad(kdata[..., 0].transpose(3, 0, 2, 1).reshape(coils, 2 * lane), ((0, 16 - coils), (0, 0)))
    dma = pltpu.SemaphoreType.DMA
    vm = pltpu.VMEM
    scratch = [
        vm((chunks, GROUP * sl, 2 * width), BF),
        vm((chunks, 2 * width, GROUP * sl), BF),
        vm((chunks, GROUP, 2 * sl, width), BF),
        vm((n_rows, 2 * lane), BF),
        vm((8 * frames, 8 * rank), BF),
        vm((2 * sl, 2 * lane), BF),
        vm((2, 2, blocks, lane), F32),
        vm((2, blocks, lane), I32),
        vm((n_rows, n_rows), BF),
        vm((n_rows, n_rows), BF),
        vm((chunks, na, nb, GROUP * nc, 2 * lane), BF),
        vm((chunks, na, nb, GROUP * nc, 2 * lane), BF),
        vm((chunks, nb, GROUP * nc, 2 * lane), BF),
        vm((chunks, nb, GROUP * nc, 2 * lane), BF),
        vm((chunks, GROUP * nc, 2 * lane), BF),
        vm((chunks, nc, GROUP * nc, 2 * lane), BF),
        vm((chunks, na, nb, GROUP * nc, 2 * lane), BF),
        vm((blocks, 1, lane), I32),
        vm((nf, 2, span, rank), BF),
        vm((nc, 16, 2 * lane), BF),
        vm((chunks, GROUP * nc, 2 * lane), F32),
        vm((GROUP * sl, 2 * width), BF),
        vm((2 * sl, 2 * lane), F32),
        vm((nf + 3, span, 4 * rank), F32),
        vm((4, 4, span, 4 * rank), F32),
        dma((24, 4)),
        dma((3, 4)),
        dma((3, 4)),
        dma((3, 4)),
        dma((3, 4)),
        dma((3, 4)),
        dma((3, 4)),
        dma((4,)),
        dma((4,)),
        dma((4, 4)),
    ]
    grad, fg = pl.pallas_call(
        functools.partial(kernel, (na, nb, nc, nf, chunks), scale),
        out_shape=(
            jax.ShapeDtypeStruct((2, slab, rank, width), F32),
            jax.ShapeDtypeStruct((span, 4 * rank), F32),
        ),
        in_specs=[pl.BlockSpec(memory_space=pltpu.VMEM)] * 6,
        out_specs=[pl.BlockSpec(memory_space=pltpu.VMEM)] * 2,
        scratch_shapes=scratch,
        compiler_params=pltpu.CompilerParams(
            collective_id=0, has_side_effects=True, vmem_limit_bytes=56 * 1024 * 1024
        ),
    )(b, m, v, l, d, table)
    grad = grad.transpose(0, 2, 1, 3)[:, :, :, None]
    fg = fg[:, : 2 * rank].reshape(span, 2, rank).transpose(1, 2, 0)
    return grad, fg


def solution(mesh):
    placed = (
        P(None, None, "cuts", "frame", None),
        P(None, None, "cuts", "frame", None),
        P(None, None, "frame"),
        P(None, "cuts"),
        P(None, None, "cuts", None, "frame"),
    )
    return jax.shard_map(
        body,
        mesh=mesh,
        in_specs=placed,
        out_specs=(P(None, None, "cuts", "frame", None), P(None, None, "frame")),
        check_vma=False,
    )
```

time: 1550 us -> 66.5 us (0.04)
  the two profiles are of different devices: /device:TPU:0 before, /device:TPU:1 now
where the time goes in v2:
time: 66.5 us; the launch traced here: 65.5 us
  Pallas kernels  58.2 us (88%)
  local copies, waits for them, and re-layouts  6.62 us (10%)
  between operations  0.69 us (1%)
    pallas_call x1, Pallas kernels, body(): pl.pallas_call(functools.partial(kernel, (na, nb, nc, nf, chunks), scale)...  58.2 us
    unnamed x10, local copies, waits for them, and re-layouts  3.2 us

profile of v2, /device:TPU:1, one launch (start us, length us, event | category | flops | bytes accessed | tf_op | source)
XLA Modules:
  0.0 65.5 jit_solution(1149471827685607966)
XLA Ops:
  0.6 0.0 copy-start.3
  0.6 0.7 %copy-done.3 = s32[64,2]{0,1:T(2,128)S(1)} copy-done((s32[64,2]{0,1:T(2,128)S(1)}, s32[64,2]{0,1:T(2,128)}, u32[]{:S(2)}) %copy-start.3) | copy-done | bytes 536
  1.3 0.6 reshape.30.l_ref
  1.9 0.7 %copy.10 = bf16[12,2,2,64]{3,2,1,0:T(2,128)(2,1)S(1)} copy(bf16[12,2,2,64]{3,2,0,1:T(2,128)(2,1)} %bitcast.25) | data formatting | bytes 12288 | tf_op jit(solution)/shard_map/transpose | solution.py:459
  2.6 0.0 copy-start.1
  2.7 0.1 reshape.31
  2.7 0.6 pad.4.d_ref
  3.3 0.0 copy-done.1
  3.4 0.0 copy-start
  3.5 0.7 %reshape.33.m_ref = f32[48,1,256]{2,1,0:T(1,128)} reshape(f32[12,2,2,256]{3,2,1,0:T(2,128)S(1)} %copy.9) | data formatting | bytes 98304 | tf_op jit(solution)/shard_map/convert_element_type | solution.py:456
  4.1 0.1 copy-done
  4.3 0.6 copy.15
  4.9 58.2 %shard_map.77 = (f32[2,2,32,256]{3,2,1,0:T(8,128)}, f32[16,128]{1,0:T(8,128)}) custom-call(bf16[2,2,32,256]{3,2,1,0:T(8,128)(2,1)} %bitcast.22, f32[48,1,256]{2,1,0:T(1,128)} %reshape.33.m_ref, bf16[2,16,32]{2,1,0:T(8,128)(2,1)} %bitcast.26, s32[1,128]{1,0:T(1,128)} %reshape.30.l_ref, bf16[16,256]{1,0:T(8,128)(2,1)} %pad.4.d_ref, ...), custom_call_target="tpu_custom_call" | custom-call | tf_op jit(solution)/shard_map/pallas_call | solution.py:499
  63.1 0.0 copy-start.2
  63.2 1.7 %copy.12 = f32[2,32,2,1,256]{4,3,2,1,0:T(1,128)} copy(f32[2,32,2,1,256]{4,1,2,0,3:T(8,128)} %bitcast.23) | data formatting | bytes 262144
  64.9 0.0 copy-done.2
  64.9 0.1 reshape.32
  64.9 0.6 copy.16
  (2 shorter events, 0.0 us)
Async XLA Ops:
  0.6 0.7 %copy-start.3 = (s32[64,2]{0,1:T(2,128)S(1)}, s32[64,2]{0,1:T(2,128)}, u32[]{:S(2)}) copy-start(s32[64,2]{0,1:T(2,128)} %param.9) | copy-start | bytes 1540
  2.6 0.7 %copy-start.1 = (bf16[2,12,2,1,256]{4,2,3,1,0:T(2,128)(2,1)S(1)}, bf16[2,12,2,1,256]{4,2,3,1,0:T(2,128)(2,1)}, u32[]{:S(2)}) copy-start(bf16[2,12,2,1,256]{4,2,3,1,0:T(2,128)(2,1)} %param.7) | copy-start | bytes 73732
  3.4 0.8 %copy-start = (bf16[2,32,2,1,256]{4,2,3,1,0:T(2,128)(2,1)S(1)}, bf16[2,32,2,1,256]{4,2,3,1,0:T(2,128)(2,1)}, u32[]{:S(2)}) copy-start(bf16[2,32,2,1,256]{4,2,3,1,0:T(2,128)(2,1)} %param.6) | copy-start | bytes 196612
  63.1 1.7 %copy-start.2 = (f32[16,128]{1,0:T(8,128)S(1)}, f32[16,128]{1,0:T(8,128)}, u32[]{:S(2)}) copy-start(f32[16,128]{1,0:T(8,128)} %get-tuple-element.5) | copy-start | bytes 24580

commit v3 on v2

v3 whole, which is shorter than its diff:
```python
import functools
import math

import jax
import jax.numpy as jnp
import numpy as np
from jax import lax
from jax.experimental import pallas as pl
from jax.experimental.pallas import tpu as pltpu
from jax.sharding import PartitionSpec as P

BF = jnp.bfloat16
F32 = jnp.float32
I32 = jnp.int32
GROUP = 4
ROWS = 4


def real_table(size, shape):
    index = np.arange(size)
    angle = (index[:, None] * index[None, :] % size) * (2.0 * math.pi / size)
    cosine, sine = np.cos(angle) / math.sqrt(size), np.sin(angle) / math.sqrt(size)
    block = np.arange(np.prod(shape)).reshape(shape).transpose(2, 0, 1).reshape(-1)
    order = (np.arange(ROWS)[:, None] + ROWS * block[None, :]).reshape(-1)
    c, s = cosine[order], sine[order]
    return np.block([[c, s], [-s, c]])


def nn(a, b):
    return jnp.dot(a, b, preferred_element_type=F32)


def nt(a, b):
    return lax.dot_general(a, b, (((1,), (1,)), ((), ())), preferred_element_type=F32)


def iota(shape, axis):
    return lax.broadcasted_iota(I32, shape, axis)


def kernel(
    dims,
    scale,
    b_hbm,
    m_hbm,
    v_hbm,
    l_hbm,
    d_hbm,
    t_hbm,
    grad_hbm,
    fg_hbm,
    bv,
    mv,
    lv,
    dv,
    t_ref,
    bf,
    mf,
    lt,
    kt,
    img,
    ht,
    hn,
    mix,
    pb,
    vbt,
    vc,
    ph,
    rowid,
    perm,
    permt,
    sx,
    xr,
    sy,
    yr,
    sz,
    zr,
    ra,
    lg,
    vg,
    kg,
    kd,
    ea,
    zg,
    gv,
    gout,
    gs,
    gz,
    gt,
    gx,
    fo,
    local,
    send,
    rx,
    ry,
    rz,
    ray,
    rax,
    slx,
    rlx,
    rlc,
    rv,
    rk,
    sgz,
    rgz,
    sgx,
    rgx,
):
    na, nb, nc, nf, chunks = dims
    coils = chunks * GROUP
    rank = b_hbm.shape[0] // 2
    slab, width = b_hbm.shape[1:]
    span = v_hbm.shape[1]
    frames = span * nf
    nab = na * nb
    blocks = nab * nc
    depth = slab * blocks
    cells = depth * ROWS
    me = lax.axis_index("cuts")
    fr = lax.axis_index("frame")
    ia, ib, ic = me // (nb * nc), (me // nc) % nb, me % nc
    ab = ia * nb + ib
    lane = 2 * frames
    sl = slab * rank
    mesh_id = pl.DeviceIdType.MESH

    def cut(a, b, c):
        return a * (nb * nc) + b * nc + c

    def peer_a(j):
        return {"cuts": cut(lax.rem(ia + j, na), ib, ic)}

    def peer_b(j):
        return {"cuts": cut(ia, lax.rem(ib + j, nb), ic)}

    def peer_c(j):
        return {"cuts": cut(ia, ib, lax.rem(ic + j, nc))}

    def peer_f(j):
        return {"frame": lax.rem(fr + j, nf)}

    def peer_ab(j):
        return {"cuts": cut(lax.rem(ia + j // nb, na), lax.rem(ib + j % nb, nb), ic)}

    def peer_cf(j):
        return {
            "cuts": cut(ia, ib, lax.rem(ic + j // nf, nc)),
            "frame": lax.rem(fr + j % nf, nf),
        }

    def remote(src, dst, s, r, who):
        return pltpu.make_async_remote_copy(
            src_ref=src, dst_ref=dst, send_sem=s, recv_sem=r, device_id=who, device_id_type=mesh_id
        )

    everyone = [peer_ab(j) for j in range(1, nab)] + [peer_cf(j) for j in range(1, nc * nf)]
    barrier = pltpu.get_barrier_semaphore()
    for who in everyone:
        pl.semaphore_signal(barrier, inc=1, device_id=who, device_id_type=mesh_id)

    loads = [
        pltpu.make_async_copy(l_hbm, lv, local.at[0]),
        pltpu.make_async_copy(b_hbm, bv, local.at[1]),
        pltpu.make_async_copy(m_hbm, mv, local.at[2]),
        pltpu.make_async_copy(t_hbm, t_ref, local.at[3]),
        pltpu.make_async_copy(v_hbm, vg.at[fr], local.at[4]),
        pltpu.make_async_copy(d_hbm, dv, local.at[5]),
    ]
    for copy in loads:
        copy.start()

    n_rows = GROUP * blocks
    out_row = iota((n_rows, n_rows), 0)
    in_row = iota((n_rows, n_rows), 1)

    def spot(r):
        return r // nc % GROUP * blocks + r % nc * nab + r // (nc * GROUP)

    perm[...] = (spot(out_row) == in_row).astype(F32).astype(BF)
    permt[...] = (spot(in_row) == out_row).astype(F32).astype(BF)

    loads[0].wait()
    row = lv[0:1, :] + lv[1:2, :] * cells
    lt[0:1, 0:frames] = row
    lt[0:1, frames:lane] = row
    lg[ic, pl.ds(ab, 1)] = lt[...][None]
    loads[1].wait()
    loads[2].wait()
    for p in range(2):
        x = bv[p * rank : (p + 1) * rank].astype(F32)
        for z in range(slab):
            bf[z, p] = x[:, z, :]
    mf[...] = mv[...].astype(F32)
    loads[3].wait()
    loads[4].wait()

    def forward(k, carry):
        for c4 in range(GROUP):
            c = k * GROUP + c4
            for z in range(slab):
                mr, mi = mf[c, z : z + 1, :], mf[coils + c, z : z + 1, :]
                br, bi = bf[z, 0], bf[z, 1]
                at = (c4 * slab + z) * rank
                img[k, at : at + rank, 0:width] = (mr * br - mi * bi).astype(BF)
                img[k, at : at + rank, width : 2 * width] = (mr * bi + mi * br).astype(BF)
        ht[k] = nt(t_ref[...], img[k]).astype(BF)
        return carry

    pl.semaphore_wait(barrier, len(everyone))

    lab = [
        remote(
            lg.at[ic, pl.ds(ab, 1)], lg.at[ic, pl.ds(ab, 1)], slx.at[j], rlx.at[j], peer_ab(j)
        )
        for j in range(1, nab)
    ]
    vcopies = [
        remote(vg.at[fr], vg.at[fr], send.at[0, j], rv.at[j], peer_f(j)) for j in range(1, nf)
    ]
    for copy in lab + vcopies:
        copy.start()
    lax.fori_loop(0, chunks, forward, 0)

    def again(k, carry):
        full = nt(img[k], t_ref[...]).astype(BF)
        for c4 in range(GROUP):
            hn[k, c4, 0:sl, :] = full[c4 * sl : (c4 + 1) * sl, 0:width]
            hn[k, c4, sl : 2 * sl, :] = full[c4 * sl : (c4 + 1) * sl, width : 2 * width]
        return carry

    lax.fori_loop(0, chunks, again, 0)
    loads[5].wait()
    kt[...] = jnp.zeros_like(kt)
    for q in range(2):
        x = dv[q * coils : (q + 1) * coils].astype(F32)
        for s in range(2):
            kt[0:coils, q * lane + s * frames : q * lane + (s + 1) * frames] = x[:, s, :]
    kg[ic] = kt[...].astype(BF)
    kcopies = [
        remote(kg.at[ic], kg.at[ic], send.at[1, j], rk.at[j], peer_c(j)) for j in range(1, nc)
    ]
    for copy in lab:
        copy.wait()
    lc = [
        remote(lg.at[ic], lg.at[ic], send.at[2, j], rlc.at[j], peer_c(j)) for j in range(1, nc)
    ]
    for copy in lc + kcopies:
        copy.start()
    for copy in vcopies:
        copy.wait()

    vt = [vg[:, p].reshape(frames, rank) for p in range(2)]
    rep = (iota((rank, 4 * rank), 0) == iota((rank, 4 * rank), 1) % rank).astype(F32).astype(BF)
    wide = [nn(vt[p], rep) for p in range(2)]
    block_of = iota((frames, 4 * rank), 1) // rank
    for blk in range(4):
        r_ = jnp.where(block_of == blk, wide[0], 0.0).astype(BF)
        i_ = jnp.where(block_of == blk, wide[1], 0.0).astype(BF)
        at = blk * frames
        vbt[at : at + frames, 0 : 4 * rank] = r_
        vbt[at : at + frames, 4 * rank : 8 * rank] = -i_
        at = (4 + blk) * frames
        vbt[at : at + frames, 0 : 4 * rank] = i_
        vbt[at : at + frames, 4 * rank : 8 * rank] = r_
    rep2 = (iota((sl, rank), 0) % rank == iota((sl, rank), 1)).astype(F32).astype(BF)
    same = iota((sl, lane), 0) // rank == iota((sl, lane), 1) // frames
    tall = [nt(rep2, jnp.concatenate([vt[p], vt[p]], 0)) for p in range(2)]
    r_ = jnp.where(same, tall[0], 0.0).astype(BF)
    i_ = jnp.where(same, tall[1], 0.0).astype(BF)
    vc[0:sl, 0:lane] = r_
    vc[0:sl, lane : 2 * lane] = i_
    vc[sl : 2 * sl, 0:lane] = -i_
    vc[sl : 2 * sl, lane : 2 * lane] = r_

    def mixing(i, carry):
        k, pair = i // 2, i % 2
        for half in range(2):
            at = half * 2 * sl

            @pl.when(pair == half)
            def _():
                lhs = jnp.concatenate(
                    [ht[k, 0:width, at : at + 2 * sl], ht[k, width : 2 * width, at : at + 2 * sl]],
                    1,
                )
                mix[i] = nt(lhs, vbt[...])

        return carry

    lax.fori_loop(0, 2 * chunks, mixing, 0)
    for copy in kcopies:
        copy.wait()
    kall = kg[...].reshape(nc * 16, 2 * lane)
    krow = iota((chunks * GROUP * nc, nc * 16), 0)
    kcol = iota((chunks * GROUP * nc, nc * 16), 1)
    pick = (krow % nc * 16 + krow // nc == kcol).astype(F32).astype(BF)
    kd[...] = nn(pick, kall).reshape(chunks, GROUP * nc, 2 * lane)
    for copy in lc:
        copy.wait()

    lo = iota((blocks, lane), 1) < frames
    both = lg[...].reshape(blocks, lane)
    zpos = me * slab + iota((blocks, lane), 1) // frames
    norm = 1.0 / math.sqrt(depth)
    for s in range(2):
        mine = lax.rem(both, cells) if s == 0 else lax.div(both, cells)
        kz = lax.rem(mine, depth)
        rowid[s] = lax.div(mine, depth)
        angle = lax.rem(kz * zpos, depth).astype(F32) * (2.0 * math.pi / depth)
        ph[s, 0] = (jnp.cos(angle) * norm).astype(BF).astype(F32)
        ph[s, 1] = (jnp.sin(angle) * -norm).astype(BF).astype(F32)

    def to_a(k, j):
        return remote(
            sx.at[k, lax.rem(ia + j, na)], xr.at[k, j], send.at[5 + k, j], rx.at[k, j], peer_a(j)
        )

    def to_b(k, j):
        return remote(
            sy.at[k, lax.rem(ib + j, nb)], yr.at[k, j], send.at[8 + k, j], ry.at[k, j], peer_b(j)
        )

    def to_c(k, j):
        return remote(sz.at[k], zr.at[k, j], send.at[11 + k, j], rz.at[k, j], peer_c(j))

    def back_b(k, j):
        return remote(
            ra.at[k, ia, ib], ra.at[k, ia, ib], send.at[14 + k, j], ray.at[k, j], peer_b(j)
        )

    def back_a(k, j):
        return remote(ra.at[k, ia], ra.at[k, ia], send.at[17 + k, j], rax.at[k, j], peer_a(j))

    def parts_of(k, carry):
        for c4 in range(GROUP):
            i, c2 = k * 2 + c4 // 2, c4 % 2
            re0, im0 = c2 * lane, (2 + c2) * lane
            got = []
            for s in range(2):
                rs = rowid[s]
                mr = mix[i, 0:blocks, re0 : re0 + lane]
                mi = mix[i, 0:blocks, im0 : im0 + lane]
                for r in range(1, ROWS):
                    here = rs == r
                    mr = jnp.where(here, mix[i, r * blocks : (r + 1) * blocks, re0 : re0 + lane], mr)
                    mi = jnp.where(here, mix[i, r * blocks : (r + 1) * blocks, im0 : im0 + lane], mi)
                pr, pi = ph[s, 0], ph[s, 1]
                got.append((pr * mr - pi * mi, pr * mi + pi * mr))
            row = c4 * blocks
            for q in range(2):
                keep = jnp.where(lo, got[0][q], got[1][q])
                fold = jnp.where(lo, got[1][q], got[0][q])
                total = keep + pltpu.roll(fold, frames, 1)
                pb[row : row + blocks, q * lane : (q + 1) * lane] = total.astype(BF)
        part = nn(perm[...], pb[...]).astype(BF)
        sx[k] = part.reshape(na, nb, GROUP * nc, 2 * lane)
        for j in range(1, na):
            to_a(k, j).start()
        return carry

    lax.fori_loop(0, chunks, parts_of, 0)

    for k in range(chunks):
        total = sx[k, ia].astype(F32)
        for j in range(1, na):
            to_a(k, j).wait()
            total = total + xr[k, j].astype(F32)
        sy[k] = total.astype(BF)
        for j in range(1, nb):
            to_b(k, j).start()
    for k in range(chunks):
        total = sy[k, ib].astype(F32)
        for j in range(1, nb):
            to_b(k, j).wait()
            total = total + yr[k, j].astype(F32)
        sz[k] = total.astype(BF)
        for j in range(1, nc):
            to_c(k, j).start()
    for k in range(chunks):
        total = sz[k].astype(F32)
        for j in range(1, nc):
            to_c(k, j).wait()
            total = total + zr[k, j].astype(F32)
        ra[k, ia, ib] = (total - kd[k]).astype(BF)
        for j in range(1, nb):
            back_b(k, j).start()
    for k in range(chunks):
        for j in range(1, nb):
            back_b(k, j).wait()
        for j in range(1, na):
            back_a(k, j).start()
    gv[...] = jnp.zeros_like(gv)

    def spread(k, carry):
        for j in range(1, na):
            back_a(k, j).wait()
        resid = nn(permt[...], ra[k].reshape(n_rows, 2 * lane))
        for c4 in range(GROUP):
            here = [
                resid[c4 * blocks : (c4 + 1) * blocks, q * lane : (q + 1) * lane] for q in range(2)
            ]
            flip = [pltpu.roll(x, frames, 1) for x in here]
            terms = []
            for s in range(2):
                xr_, xi_ = [
                    jnp.where(lo, a, b) if s == 0 else jnp.where(lo, b, a)
                    for a, b in zip(here, flip)
                ]
                pr, pi = ph[s, 0], ph[s, 1]
                terms.append((xr_ * pr + xi_ * pi, xi_ * pr - xr_ * pi))
            for r in range(ROWS):
                m0, m1 = rowid[0] == r, rowid[1] == r
                for q in range(2):
                    ea[k, c4, r * blocks : (r + 1) * blocks, q * lane : (q + 1) * lane] = (
                        jnp.where(m0, terms[0][q], 0.0) + jnp.where(m1, terms[1][q], 0.0)
                    ).astype(BF)
            gv[...] += nn(hn[k, c4], ea[k, c4])
        return carry

    lax.fori_loop(0, chunks, spread, 0)

    own = {}
    for p in range(2):
        for q in range(2):
            first = gv[p * sl : p * sl + rank, q * lane : (q + 1) * lane]
            second = gv[p * sl + rank : (p + 1) * sl, q * lane : (q + 1) * lane]
            own[p, q] = first + pltpu.roll(second, frames, 1)
    gre = (own[0, 0] + own[1, 1]) * scale
    gim = (own[0, 1] - own[1, 0]) * scale
    turned = jnp.transpose(jnp.concatenate([gre, gim, gre, gim], 0))
    half = span // 2
    first_half = iota((half, 4 * rank), 1) < 2 * rank
    for f in range(nf):
        gs[f] = jnp.where(
            first_half,
            turned[f * span : f * span + half],
            turned[f * span + half : (f + 1) * span],
        ).astype(BF)
    gcf = [
        remote(gs.at[lax.rem(fr + j % nf, nf)], gz.at[j], sgz.at[j], rgz.at[j], peer_cf(j))
        for j in range(1, nc * nf)
    ]
    for copy in gcf:
        copy.start()

    def backward(k, carry):
        for c4 in range(GROUP):
            zc = nt(vc[...], ea[k, c4]).astype(BF)
            zg[k, c4 * sl : (c4 + 1) * sl, 0:width] = zc[0:sl]
            zg[k, c4 * sl : (c4 + 1) * sl, width : 2 * width] = zc[sl : 2 * sl]
        back = nn(zg[k], t_ref[...])
        out = list(carry)
        for z in range(slab):
            re, im = out[2 * z], out[2 * z + 1]
            for c4 in range(GROUP):
                c = k * GROUP + c4
                mr, mi = mf[c, z : z + 1, :], mf[coils + c, z : z + 1, :]
                at = (c4 * slab + z) * rank
                br = back[at : at + rank, 0:width]
                bi = back[at : at + rank, width : 2 * width]
                re = re + mr * br + mi * bi
                im = im + mr * bi - mi * br
            out[2 * z], out[2 * z + 1] = re, im
        return tuple(out)

    zero = jnp.zeros((rank, width), F32)
    out = lax.fori_loop(0, chunks, backward, (zero,) * (2 * slab))
    for z in range(slab):
        for p in range(2):
            gout[p * rank : (p + 1) * rank, z] = out[2 * z + p].reshape(rank, 1, width)
    store = pltpu.make_async_copy(gout, grad_hbm, local.at[6])
    store.start()

    total = gs[fr].astype(F32)
    for j, copy in enumerate(gcf):
        copy.wait()
        total = total + gz[j + 1].astype(F32)
    gt[...] = total
    gab = [remote(gt, gx.at[j], sgx.at[j], rgx.at[j], peer_ab(j)) for j in range(1, nab)]
    for copy in gab:
        copy.start()
    for j, copy in enumerate(gab):
        copy.wait()
        total = total + gx[j + 1]
    for q in range(2):
        for h in range(2):
            at = (2 * h + q) * rank
            fo[q, h * half : (h + 1) * half, :] = total[:, at : at + rank]
    last = pltpu.make_async_copy(fo, fg_hbm, local.at[7])
    last.start()
    last.wait()
    store.wait()


SHAPES = {64: (4, 4, 4), 8: (2, 2, 2)}


def body(basis, coil_maps, factors, lines, kdata):
    n_cuts = lax.axis_size("cuts")
    nf = lax.axis_size("frame")
    na, nb, nc = SHAPES[n_cuts]
    rank, slab, width = basis.shape[1], basis.shape[2], basis.shape[4]
    coils = coil_maps.shape[1]
    chunks = coils // GROUP
    span = factors.shape[2]
    lpd = lines.shape[1]
    frames = span * nf
    lane = 2 * frames
    sl = slab * rank
    blocks = n_cuts
    n_rows = GROUP * blocks
    scale = 1.0 / math.sqrt(coils * lpd * n_cuts * basis.shape[3] * nf)
    table = jnp.asarray(real_table(width, (na, nb, nc)), BF)
    b = basis.transpose(0, 1, 3, 2, 4).reshape(2 * rank, slab, width)
    m = coil_maps.transpose(0, 1, 3, 2, 4).reshape(2 * coils, slab, width)
    v = factors.transpose(0, 2, 1)
    l = lines.T
    d = kdata.transpose(0, 3, 4, 2, 1).reshape(2 * coils, lpd, frames)
    dma = pltpu.SemaphoreType.DMA
    vm = pltpu.VMEM
    slabs = (chunks, na, nb, GROUP * nc, 2 * lane)
    scratch = [
        vm(b.shape, BF),
        vm(m.shape, BF),
        vm(l.shape, I32),
        vm(d.shape, BF),
        vm(table.shape, BF),
        vm((slab, 2, rank, width), F32),
        vm(m.shape, F32),
        vm((1, lane), I32),
        vm((16, 2 * lane), F32),
        vm((chunks, GROUP * sl, 2 * width), BF),
        vm((chunks, 2 * width, GROUP * sl), BF),
        vm((chunks, GROUP, 2 * sl, width), BF),
        vm((2 * chunks, width, 4 * lane), F32),
        vm((n_rows, 2 * lane), BF),
        vm((8 * frames, 8 * rank), BF),
        vm((2 * sl, 2 * lane), BF),
        vm((2, 2, blocks, lane), F32),
        vm((2, blocks, lane), I32),
        vm((n_rows, n_rows), BF),
        vm((n_rows, n_rows), BF),
        vm(slabs, BF),
        vm((chunks, na) + slabs[2:], BF),
        vm((chunks,) + slabs[2:], BF),
        vm((chunks,) + slabs[2:], BF),
        vm((chunks,) + slabs[3:], BF),
        vm((chunks, nc) + slabs[3:], BF),
        vm(slabs, BF),
        vm((nc, na * nb, 1, lane), I32),
        vm((nf, 2, span, rank), BF),
        vm((nc, 16, 2 * lane), BF),
        vm((chunks,) + slabs[3:], F32),
        vm((chunks, GROUP, width, 2 * lane), BF),
        vm((chunks, GROUP * sl, 2 * width), BF),
        vm((2 * sl, 2 * lane), F32),
        vm((2 * rank, slab, 1, width), F32),
        vm((nf, span // 2, 4 * rank), BF),
        vm((nc * nf, span // 2, 4 * rank), BF),
        vm((span // 2, 4 * rank), F32),
        vm((na * nb, span // 2, 4 * rank), F32),
        vm((2, span, rank), F32),
        dma((8,)),
        dma((20, 4)),
        dma((3, 4)),
        dma((3, 4)),
        dma((3, 4)),
        dma((3, 4)),
        dma((3, 4)),
        dma((na * nb,)),
        dma((na * nb,)),
        dma((4,)),
        dma((4,)),
        dma((4,)),
        dma((nc * nf,)),
        dma((nc * nf,)),
        dma((na * nb,)),
        dma((na * nb,)),
    ]
    grad, fg = pl.pallas_call(
        functools.partial(kernel, (na, nb, nc, nf, chunks), scale),
        out_shape=(
            jax.ShapeDtypeStruct((2 * rank, slab, 1, width), F32),
            jax.ShapeDtypeStruct((2, span, rank), F32),
        ),
        in_specs=[pl.BlockSpec(memory_space=pl.ANY)] * 6,
        out_specs=[pl.BlockSpec(memory_space=pl.ANY)] * 2,
        scratch_shapes=scratch,
        compiler_params=pltpu.CompilerParams(
            collective_id=0, has_side_effects=True, vmem_limit_bytes=56 * 1024 * 1024
        ),
    )(b, m, v, l, d, table)
    return grad.reshape(basis.shape), fg.transpose(0, 2, 1)


def solution(mesh):
    placed = (
        P(None, None, "cuts", "frame", None),
        P(None, None, "cuts", "frame", None),
        P(None, None, "frame"),
        P(None, "cuts"),
        P(None, None, "cuts", None, "frame"),
    )
    return jax.shard_map(
        body,
        mesh=mesh,
        in_specs=placed,
        out_specs=(P(None, None, "cuts", "frame", None), P(None, None, "frame")),
        check_vma=False,
    )
```

time: 66.5 us -> 56.3 us (0.85); the launches traced: 65.5 us -> 56.2 us
  Pallas kernels: 58.2 us -> 53.4 us
  local copies, waits for them, and re-layouts: 6.62 us -> 2.18 us
    pallas_call x1, Pallas kernels: 58.2 us -> 53.4 us  [body(): pl.pallas_call(functools.partial(kernel, (na, nb, nc, nf, chunks), scale)...]
    reshape x4 -> x0, local copies, waits for them, and re-layouts: 1.39 us -> none  [the longest x2 0.69 us: body(): fg = fg[:, :2 * rank].reshape(span, 2, rank).transpose(1, 2, 0)]
    unnamed x10 -> x4, local copies, waits for them, and re-layouts: 3.2 us -> 2.18 us
    transpose x1 -> x0, local copies, waits for them, and re-layouts: 0.72 us -> none  [body(): kdata[..., 0].transpose(3, 0, 2, 1).reshape(coils, 2 * lane)]
    convert_element_type x2 -> x0, local copies, waits for them, and re-layouts: 0.71 us -> none  [body(): coil_maps[:, :, :, 0].transpose(1, 2, 0, 3)]
where the time goes in v3:
time: 56.3 us; the launch traced here: 56.2 us
  Pallas kernels  53.4 us (95%)
  local copies, waits for them, and re-layouts  2.18 us (4%)
  between operations  0.65 us (1%)
    pallas_call x1, Pallas kernels, body(): pl.pallas_call(functools.partial(kernel, (na, nb, nc, nf, chunks), scale)...  53.4 us
    unnamed x4, local copies, waits for them, and re-layouts  2.18 us

profile of v3, /device:TPU:1, one launch (start us, length us, event | category | flops | bytes accessed | tf_op | source)
XLA Modules:
  0.0 56.2 jit_solution(17747797663949247195)
XLA Ops:
  0.6 53.4 %shard_map.77 = (f32[64,2,1,256]{3,2,1,0:T(1,128)}, f32[2,16,32]{2,1,0:T(8,128)}) custom-call(bf16[64,2,256]{2,1,0:T(2,128)(2,1)} %bitcast.10, bf16[24,2,256]{2,1,0:T(2,128)(2,1)} %bitcast.11, bf16[2,16,32]{2,1,0:T(8,128)(2,1)} %bitcast.14, s32[2,64]{1,0:T(2,128)} %bitcast.15, bf16[24,2,64]{2,1,0:T(2,128)(2,1)} %bitcast.13, bf16[512,512]{1,0:T(8,128)(2,1)} %constant.2.clone.t_hbm), custom_call_target="tpu_custom_call" | custom-call | tf_op jit(solution)/shard_map/pallas_call | solution.py:580
  54.0 0.0 copy-start
  54.0 1.6 %copy.10 = f32[2,32,2,1,256]{4,3,2,1,0:T(1,128)} copy(f32[2,32,2,1,256]{4,3,2,1,0:T(1,128)} %bitcast.9) | data formatting | bytes 262144
  55.6 0.0 copy-done
  55.6 0.6 %copy.11 = f32[2,32,16]{1,2,0:T(8,128)} copy(f32[2,32,16]{1,2,0:T(8,128)S(1)} %bitcast.12) | data formatting | bytes 8192
Async XLA Ops:
  54.0 1.6 %copy-start = (f32[2,16,32]{2,1,0:T(8,128)S(1)}, f32[2,16,32]{2,1,0:T(8,128)}, u32[]{:S(2)}) copy-start(f32[2,16,32]{2,1,0:T(8,128)} %get-tuple-element.5) | copy-start | bytes 12292

commit v4 on v3

v4 whole, which is shorter than its diff:
```python
import functools
import math

import jax
import jax.numpy as jnp
import numpy as np
from jax import lax
from jax.experimental import pallas as pl
from jax.experimental.pallas import tpu as pltpu
from jax.sharding import PartitionSpec as P

BF = jnp.bfloat16
F32 = jnp.float32
I32 = jnp.int32
GROUP = 4
ROWS = 4


def real_table(size, shape):
    index = np.arange(size)
    angle = (index[:, None] * index[None, :] % size) * (2.0 * math.pi / size)
    cosine, sine = np.cos(angle) / math.sqrt(size), np.sin(angle) / math.sqrt(size)
    whole = np.stack([np.concatenate([cosine, sine], 1), np.concatenate([-sine, cosine], 1)])
    whole = whole.reshape((2,) + tuple(shape) + (ROWS, 2 * size))
    first = whole.transpose(1, 2, 0, 4, 3, 5).reshape(2 * size, 2 * size)
    second = whole.transpose(0, 4, 3, 1, 2, 5).reshape(2 * size, 2 * size)
    return first, second


def nn(a, b):
    return jnp.dot(a, b, preferred_element_type=F32)


def nt(a, b):
    return lax.dot_general(a, b, (((1,), (1,)), ((), ())), preferred_element_type=F32)


def iota(shape, axis):
    return lax.broadcasted_iota(I32, shape, axis)


def kernel(
    dims,
    scale,
    b_hbm,
    m_hbm,
    v_hbm,
    l_hbm,
    d_hbm,
    t_hbm,
    t2_hbm,
    grad_hbm,
    fg_hbm,
    bv,
    mv,
    lv,
    dv,
    t_ref,
    t2_ref,
    bf,
    mf,
    lt,
    l8,
    kt,
    img,
    ht,
    hr,
    hn,
    vbt,
    vc,
    pf,
    ph,
    rowid,
    permt,
    zr,
    ra,
    lg,
    vg,
    kg,
    kd,
    ea,
    zg,
    gv,
    gout,
    gs,
    gz,
    gx,
    fo,
    local,
    send,
    recv,
):
    na, nb, nc, nf, chunks = dims
    coils = chunks * GROUP
    rank = b_hbm.shape[0] // 2
    slab, width = b_hbm.shape[1:]
    span = v_hbm.shape[1]
    frames = span * nf
    nab = na * nb
    blocks = nab * nc
    depth = slab * blocks
    cells = depth * ROWS
    me = lax.axis_index("cuts")
    fr = lax.axis_index("frame")
    ia, ib, ic = me // (nb * nc), (me // nc) % nb, me % nc
    ab = ia * nb + ib
    lane = 2 * frames
    sl = slab * rank
    mesh_id = pl.DeviceIdType.MESH

    def cut(a, b, c):
        return a * (nb * nc) + b * nc + c

    def peer_c(j):
        return {"cuts": cut(ia, ib, lax.rem(ic + j, nc))}

    def peer_f(j):
        return {"frame": lax.rem(fr + j, nf)}

    def peer_ab(j):
        return {"cuts": cut(lax.rem(ia + j // nb, na), lax.rem(ib + j % nb, nb), ic)}

    def peer_cf(j):
        return {
            "cuts": cut(ia, ib, lax.rem(ic + j // nf, nc)),
            "frame": lax.rem(fr + j % nf, nf),
        }

    def remote(src, dst, s, r, who):
        return pltpu.make_async_remote_copy(
            src_ref=src, dst_ref=dst, send_sem=s, recv_sem=r, device_id=who, device_id_type=mesh_id
        )

    everyone = [peer_ab(j) for j in range(1, nab)] + [peer_cf(j) for j in range(1, nc * nf)]
    barrier = pltpu.get_barrier_semaphore()
    for who in everyone:
        pl.semaphore_signal(barrier, inc=1, device_id=who, device_id_type=mesh_id)

    def settle(block, at):
        pltpu.make_async_copy(block, block, send.at[at]).wait()
        pltpu.make_async_copy(block, block, recv.at[at]).wait()

    loads = [
        pltpu.make_async_copy(l_hbm, lv, local.at[0]),
        pltpu.make_async_copy(b_hbm, bv, local.at[1]),
        pltpu.make_async_copy(m_hbm, mv, local.at[2]),
        pltpu.make_async_copy(t_hbm, t_ref, local.at[3]),
        pltpu.make_async_copy(v_hbm, vg.at[fr], local.at[4]),
        pltpu.make_async_copy(d_hbm, dv, local.at[5]),
        pltpu.make_async_copy(t2_hbm, t2_ref, local.at[6]),
    ]
    for copy in loads:
        copy.start()
    loads[0].wait()
    row = lv[0:1, :] + lv[1:2, :] * cells
    lt[0:1, 0:frames] = row
    lt[0:1, frames:lane] = row
    lg[ic, pl.ds(ab, 1)] = lt[...][None]
    loads[1].wait()
    loads[2].wait()
    for p in range(2):
        x = bv[p * rank : (p + 1) * rank].astype(F32)
        for z in range(slab):
            bf[z, p] = x[:, z, :]
    mf[...] = mv[...].astype(F32)
    loads[3].wait()
    loads[4].wait()

    def forward(k, carry):
        for c4 in range(GROUP):
            c = k * GROUP + c4
            for z in range(slab):
                mr, mi = mf[c, z : z + 1, :], mf[coils + c, z : z + 1, :]
                br, bi = bf[z, 0], bf[z, 1]
                at = (c4 * slab + z) * rank
                img[k, at : at + rank, 0:width] = (mr * br - mi * bi).astype(BF)
                img[k, at : at + rank, width : 2 * width] = (mr * bi + mi * br).astype(BF)
        ht[k] = nt(t_ref[...], img[k]).astype(BF).reshape(nab, 2, ROWS * nc, GROUP * sl)
        hr[k, ab] = ht[k, ab]
        return carry

    lax.fori_loop(0, chunks, forward, 0)

    pl.semaphore_wait(barrier, len(everyone))

    for j in range(1, nc):
        own_line = lg.at[ic, pl.ds(ab, 1)]
        remote(own_line, own_line, send.at[0], recv.at[0], peer_c(j)).start()
    for k in range(chunks):
        for j in range(1, nab):
            to = lax.rem(ia + j // nb, na) * nb + lax.rem(ib + j % nb, nb)
            remote(
                ht.at[k, to], hr.at[k, ab], send.at[1 + k], recv.at[1 + k], peer_ab(j)
            ).start()
    for j in range(1, nf):
        remote(vg.at[fr], vg.at[fr], send.at[4], recv.at[4], peer_f(j)).start()
    loads[5].wait()
    kt[...] = jnp.zeros_like(kt)
    for q in range(2):
        x = dv[q * coils : (q + 1) * coils].astype(F32)
        for s in range(2):
            kt[0:coils, q * lane + s * frames : q * lane + (s + 1) * frames] = x[:, s, :]
    kg[ic] = kt[...].astype(BF)
    for j in range(1, nc):
        remote(kg.at[ic], kg.at[ic], send.at[5], recv.at[5], peer_c(j)).start()
    loads[6].wait()

    def again(k, carry):
        full = nt(img[k], t2_ref[...]).astype(BF)
        for c4 in range(GROUP):
            hn[k, c4, 0:sl, :] = full[c4 * sl : (c4 + 1) * sl, 0:width]
            hn[k, c4, sl : 2 * sl, :] = full[c4 * sl : (c4 + 1) * sl, width : 2 * width]
        return carry

    lax.fori_loop(0, chunks, again, 0)
    settle(lg.at[pl.ds(0, nc - 1), pl.ds(0, 1)], 0)
    for j in range(1, nab):
        mine = lg.at[:, pl.ds(ab, 1)]
        remote(mine, mine, send.at[6], recv.at[6], peer_ab(j)).start()
    pair_rows = 2 * nc
    l8[0:nc] = lg[:, ab]
    l8[nc:pair_rows] = lg[:, ab]
    both = l8[...].reshape(pair_rows, lane)
    norm = 1.0 / math.sqrt(depth)
    odd = iota((pair_rows, lane), 0) // nc
    zlane = iota((pair_rows, lane), 1) // frames
    upper = []
    for s in range(2):
        mine = lax.rem(both, cells) if s == 0 else lax.div(both, cells)
        kz = lax.rem(mine, depth)
        r = lax.div(mine, depth)
        upper.append(r >= 2)
        here = lax.rem(r, 2) == odd
        for i in range(nab):
            zpos = (i * nc + ic) * slab + zlane
            angle = lax.rem(kz * zpos, depth).astype(F32) * (2.0 * math.pi / depth)
            pf[s, 0, i] = jnp.where(here, (jnp.cos(angle) * norm).astype(BF).astype(F32), 0.0)
            pf[s, 1, i] = jnp.where(here, (jnp.sin(angle) * -norm).astype(BF).astype(F32), 0.0)
    settle(vg.at[pl.ds(0, nf - 1)], 4)

    vt = [vg[:, p].reshape(frames, rank) for p in range(2)]
    rep = (iota((rank, 4 * rank), 0) == iota((rank, 4 * rank), 1) % rank).astype(F32).astype(BF)
    wide = [nn(vt[p], rep) for p in range(2)]
    block_of = iota((frames, 4 * rank), 1) // rank
    for blk in range(4):
        r_ = jnp.where(block_of == blk, wide[0], 0.0).astype(BF)
        i_ = jnp.where(block_of == blk, wide[1], 0.0).astype(BF)
        at = blk * frames
        vbt[at : at + frames, 0 : 4 * rank] = r_
        vbt[at : at + frames, 4 * rank : 8 * rank] = -i_
        at = (4 + blk) * frames
        vbt[at : at + frames, 0 : 4 * rank] = i_
        vbt[at : at + frames, 4 * rank : 8 * rank] = r_
    rep2 = (iota((sl, rank), 0) % rank == iota((sl, rank), 1)).astype(F32).astype(BF)
    same = iota((sl, lane), 0) // rank == iota((sl, lane), 1) // frames
    tall = [nt(rep2, jnp.concatenate([vt[p], vt[p]], 0)) for p in range(2)]
    r_ = jnp.where(same, tall[0], 0.0).astype(BF)
    i_ = jnp.where(same, tall[1], 0.0).astype(BF)
    vc[0:sl, 0:lane] = r_
    vc[0:sl, lane : 2 * lane] = i_
    vc[sl : 2 * sl, 0:lane] = -i_
    vc[sl : 2 * sl, lane : 2 * lane] = r_
    n_rows = GROUP * blocks
    out_row = iota((n_rows, n_rows), 0)
    in_row = iota((n_rows, n_rows), 1)
    spot = in_row // nc % GROUP * blocks + in_row % nc * nab + in_row // (nc * GROUP)
    permt[...] = (spot == out_row).astype(F32).astype(BF)
    settle(kg.at[pl.ds(0, nc - 1)], 5)
    kall = kg[...].reshape(nc * 16, 2 * lane)
    krow = iota((chunks * GROUP * nc, nc * 16), 0)
    kcol = iota((chunks * GROUP * nc, nc * 16), 1)
    pick = (krow % nc * 16 + krow // nc == kcol).astype(F32).astype(BF)
    kd[...] = nn(pick, kall).reshape(chunks, GROUP * nc, 2 * lane)
    lo8 = iota((pair_rows, lane), 1) < frames
    top = iota((pair_rows, lane), 0) < nc

    def parts_of(k, carry):
        settle(hr.at[k, pl.ds(0, nab - 1)], 1 + k)
        tiles = []
        for pair in range(GROUP // 2):
            at = pair * 2 * sl
            lhs = jnp.concatenate(
                [hr[k, :, p, :, at : at + 2 * sl].reshape(width, 2 * sl) for p in range(2)], 1
            )
            mixed = nt(lhs, vbt[...]).reshape(nab, ROWS * nc, 4 * lane)
            totals = []
            for c2 in range(2):
                re0, im0 = c2 * lane, (2 + c2) * lane
                got = []
                for s in range(2):
                    mr = jnp.where(
                        upper[s][None],
                        mixed[:, pair_rows:, re0 : re0 + lane],
                        mixed[:, :pair_rows, re0 : re0 + lane],
                    )
                    mi = jnp.where(
                        upper[s][None],
                        mixed[:, pair_rows:, im0 : im0 + lane],
                        mixed[:, :pair_rows, im0 : im0 + lane],
                    )
                    pr, pi = pf[s, 0], pf[s, 1]
                    got.append((jnp.sum(pr * mr - pi * mi, 0), jnp.sum(pr * mi + pi * mr, 0)))
                both_q = []
                for q in range(2):
                    keep = jnp.where(lo8, got[0][q], got[1][q])
                    fold = jnp.where(lo8, got[1][q], got[0][q])
                    total = keep + pltpu.roll(fold, frames, 1)
                    both_q.append(total + pltpu.roll(total, nc, 0))
                totals.append(both_q)
            tiles.append(
                jnp.concatenate([jnp.where(top, totals[0][q], totals[1][q]) for q in range(2)], 1)
            )
        zr[k, ic] = jnp.concatenate(tiles, 0).astype(BF)
        for j in range(1, nc):
            remote(
                zr.at[k, ic], zr.at[k, ic], send.at[7 + k], recv.at[7 + k], peer_c(j)
            ).start()
        return carry

    lax.fori_loop(0, chunks, parts_of, 0)
    settle(lg.at[:, pl.ds(0, nab - 1)], 6)
    lo = iota((blocks, lane), 1) < frames
    both = lg[...].reshape(blocks, lane)
    zpos = me * slab + iota((blocks, lane), 1) // frames
    for s in range(2):
        mine = lax.rem(both, cells) if s == 0 else lax.div(both, cells)
        kz = lax.rem(mine, depth)
        rowid[s] = lax.div(mine, depth)
        angle = lax.rem(kz * zpos, depth).astype(F32) * (2.0 * math.pi / depth)
        ph[s, 0] = (jnp.cos(angle) * norm).astype(BF).astype(F32)
        ph[s, 1] = (jnp.sin(angle) * -norm).astype(BF).astype(F32)
    for k in range(chunks):
        settle(zr.at[k, pl.ds(0, nc - 1)], 7 + k)
        total = zr[k, 0].astype(F32)
        for j in range(1, nc):
            total = total + zr[k, j].astype(F32)
        ra[k, ab] = (total - kd[k]).astype(BF)
        for j in range(1, nab):
            remote(
                ra.at[k, ab], ra.at[k, ab], send.at[10 + k], recv.at[10 + k], peer_ab(j)
            ).start()
    gv[...] = jnp.zeros_like(gv)

    def spread(k, carry):
        settle(ra.at[k, pl.ds(0, nab - 1)], 10 + k)
        resid = nn(permt[...], ra[k].reshape(n_rows, 2 * lane))
        for c4 in range(GROUP):
            here = [
                resid[c4 * blocks : (c4 + 1) * blocks, q * lane : (q + 1) * lane] for q in range(2)
            ]
            flip = [pltpu.roll(x, frames, 1) for x in here]
            terms = []
            for s in range(2):
                xr_, xi_ = [
                    jnp.where(lo, a, b) if s == 0 else jnp.where(lo, b, a)
                    for a, b in zip(here, flip)
                ]
                pr, pi = ph[s, 0], ph[s, 1]
                terms.append((xr_ * pr + xi_ * pi, xi_ * pr - xr_ * pi))
            for r in range(ROWS):
                m0, m1 = rowid[0] == r, rowid[1] == r
                for q in range(2):
                    ea[k, c4, r * blocks : (r + 1) * blocks, q * lane : (q + 1) * lane] = (
                        jnp.where(m0, terms[0][q], 0.0) + jnp.where(m1, terms[1][q], 0.0)
                    ).astype(BF)
            gv[...] += nn(hn[k, c4], ea[k, c4])
        return carry

    lax.fori_loop(0, chunks, spread, 0)

    own = {}
    for p in range(2):
        for q in range(2):
            first = gv[p * sl : p * sl + rank, q * lane : (q + 1) * lane]
            second = gv[p * sl + rank : (p + 1) * sl, q * lane : (q + 1) * lane]
            own[p, q] = first + pltpu.roll(second, frames, 1)
    gre = (own[0, 0] + own[1, 1]) * scale
    gim = (own[0, 1] - own[1, 0]) * scale
    turned = jnp.transpose(jnp.concatenate([gre, gim, gre, gim], 0))
    half = span // 2
    first_half = iota((half, 4 * rank), 1) < 2 * rank
    for f in range(nf):
        gs[f] = jnp.where(
            first_half,
            turned[f * span : f * span + half],
            turned[f * span + half : (f + 1) * span],
        ).astype(BF)
    spot_cf = ic * nf + fr
    gz[spot_cf] = gs[fr]
    for j in range(1, nc * nf):
        remote(
            gs.at[lax.rem(fr + j % nf, nf)], gz.at[spot_cf], send.at[13], recv.at[13], peer_cf(j)
        ).start()

    def backward(k, carry):
        for c4 in range(GROUP):
            zc = nt(vc[...], ea[k, c4]).astype(BF)
            zg[k, c4 * sl : (c4 + 1) * sl, 0:width] = zc[0:sl]
            zg[k, c4 * sl : (c4 + 1) * sl, width : 2 * width] = zc[sl : 2 * sl]
        back = nn(zg[k], t2_ref[...])
        out = list(carry)
        for z in range(slab):
            re, im = out[2 * z], out[2 * z + 1]
            for c4 in range(GROUP):
                c = k * GROUP + c4
                mr, mi = mf[c, z : z + 1, :], mf[coils + c, z : z + 1, :]
                at = (c4 * slab + z) * rank
                br = back[at : at + rank, 0:width]
                bi = back[at : at + rank, width : 2 * width]
                re = re + mr * br + mi * bi
                im = im + mr * bi - mi * br
            out[2 * z], out[2 * z + 1] = re, im
        return tuple(out)

    zero = jnp.zeros((rank, width), F32)
    out = lax.fori_loop(0, chunks, backward, (zero,) * (2 * slab))
    for z in range(slab):
        for p in range(2):
            gout[p * rank : (p + 1) * rank, z] = out[2 * z + p].reshape(rank, 1, width)
    store = pltpu.make_async_copy(gout, grad_hbm, local.at[7])
    store.start()

    settle(gz.at[pl.ds(0, nc * nf - 1)], 13)
    gx[ab] = jnp.sum(gz[...].astype(F32), 0)
    for j in range(1, nab):
        remote(gx.at[ab], gx.at[ab], send.at[14], recv.at[14], peer_ab(j)).start()
    settle(gx.at[pl.ds(0, nab - 1)], 14)
    total = jnp.sum(gx[...], 0)
    for q in range(2):
        for h in range(2):
            at = (2 * h + q) * rank
            fo[q, h * half : (h + 1) * half, :] = total[:, at : at + rank]
    last = pltpu.make_async_copy(fo, fg_hbm, local.at[8])
    last.start()
    last.wait()
    store.wait()


SHAPES = {64: (4, 4, 4), 8: (2, 2, 2)}


def body(basis, coil_maps, factors, lines, kdata):
    n_cuts = lax.axis_size("cuts")
    nf = lax.axis_size("frame")
    na, nb, nc = SHAPES[n_cuts]
    rank, slab, width = basis.shape[1], basis.shape[2], basis.shape[4]
    coils = coil_maps.shape[1]
    chunks = coils // GROUP
    span = factors.shape[2]
    lpd = lines.shape[1]
    frames = span * nf
    lane = 2 * frames
    sl = slab * rank
    blocks = n_cuts
    n_rows = GROUP * blocks
    scale = 1.0 / math.sqrt(coils * lpd * n_cuts * basis.shape[3] * nf)
    table, table2 = (jnp.asarray(x, BF) for x in real_table(width, (na, nb, nc)))
    b = basis.transpose(0, 1, 3, 2, 4).reshape(2 * rank, slab, width)
    m = coil_maps.transpose(0, 1, 3, 2, 4).reshape(2 * coils, slab, width)
    v = factors.transpose(0, 2, 1)
    l = lines.T
    d = kdata.transpose(0, 3, 4, 2, 1).reshape(2 * coils, lpd, frames)
    dma = pltpu.SemaphoreType.DMA
    vm = pltpu.VMEM
    nab = na * nb
    scratch = [
        vm(b.shape, BF),
        vm(m.shape, BF),
        vm(l.shape, I32),
        vm(d.shape, BF),
        vm(table.shape, BF),
        vm(table.shape, BF),
        vm((slab, 2, rank, width), F32),
        vm(m.shape, F32),
        vm((1, lane), I32),
        vm((2 * nc, 1, lane), I32),
        vm((16, 2 * lane), F32),
        vm((chunks, GROUP * sl, 2 * width), BF),
        vm((chunks, nab, 2, ROWS * nc, GROUP * sl), BF),
        vm((chunks, nab, 2, ROWS * nc, GROUP * sl), BF),
        vm((chunks, GROUP, 2 * sl, width), BF),
        vm((8 * frames, 8 * rank), BF),
        vm((2 * sl, 2 * lane), BF),
        vm((2, 2, nab, 2 * nc, lane), F32),
        vm((2, 2, blocks, lane), F32),
        vm((2, blocks, lane), I32),
        vm((n_rows, n_rows), BF),
        vm((chunks, nc, GROUP * nc, 2 * lane), BF),
        vm((chunks, nab, GROUP * nc, 2 * lane), BF),
        vm((nc, nab, 1, lane), I32),
        vm((nf, 2, span, rank), BF),
        vm((nc, 16, 2 * lane), BF),
        vm((chunks, GROUP * nc, 2 * lane), F32),
        vm((chunks, GROUP, width, 2 * lane), BF),
        vm((chunks, GROUP * sl, 2 * width), BF),
        vm((2 * sl, 2 * lane), F32),
        vm((2 * rank, slab, 1, width), F32),
        vm((nf, span // 2, 4 * rank), BF),
        vm((nc * nf, span // 2, 4 * rank), BF),
        vm((nab, span // 2, 4 * rank), F32),
        vm((2, span, rank), F32),
        dma((9,)),
        dma((15,)),
        dma((15,)),
    ]
    grad, fg = pl.pallas_call(
        functools.partial(kernel, (na, nb, nc, nf, chunks), scale),
        out_shape=(
            jax.ShapeDtypeStruct((2 * rank, slab, 1, width), F32),
            jax.ShapeDtypeStruct((2, span, rank), F32),
        ),
        in_specs=[pl.BlockSpec(memory_space=pl.ANY)] * 7,
        out_specs=[pl.BlockSpec(memory_space=pl.ANY)] * 2,
        scratch_shapes=scratch,
        compiler_params=pltpu.CompilerParams(
            collective_id=0, has_side_effects=True, vmem_limit_bytes=56 * 1024 * 1024
        ),
    )(b, m, v, l, d, table, table2)
    return grad.reshape(basis.shape), fg.transpose(0, 2, 1)


def solution(mesh):
    placed = (
        P(None, None, "cuts", "frame", None),
        P(None, None, "cuts", "frame", None),
        P(None, None, "frame"),
        P(None, "cuts"),
        P(None, None, "cuts", None, "frame"),
    )
    return jax.shard_map(
        body,
        mesh=mesh,
        in_specs=placed,
        out_specs=(P(None, None, "cuts", "frame", None), P(None, None, "frame")),
        check_vma=False,
    )
```

time: 56.3 us -> 46.9 us (0.83)
  Pallas kernels: 53.4 us -> 44 us
    pallas_call x1, Pallas kernels: 53.4 us -> 44 us  [body(): pl.pallas_call(functools.partial(kernel, (na, nb, nc, nf, chunks), scale)...]
where the time goes in v4:
time: 46.9 us; the launch traced here: 46.8 us
  Pallas kernels  44 us (94%)
  local copies, waits for them, and re-layouts  2.18 us (5%)
  between operations  0.65 us (1%)
    pallas_call x1, Pallas kernels, body(): pl.pallas_call(functools.partial(kernel, (na, nb, nc, nf, chunks), scale)...  44 us
    unnamed x4, local copies, waits for them, and re-layouts  2.18 us

profile of v4, /device:TPU:1, one launch (start us, length us, event | category | flops | bytes accessed | tf_op | source)
XLA Modules:
  0.0 46.8 jit_solution(12041827466063786641)
XLA Ops:
  0.6 44.0 %shard_map.86 = (f32[64,2,1,256]{3,2,1,0:T(1,128)}, f32[2,16,32]{2,1,0:T(8,128)}) custom-call(bf16[64,2,256]{2,1,0:T(2,128)(2,1)} %bitcast.10, bf16[24,2,256]{2,1,0:T(2,128)(2,1)} %bitcast.11, bf16[2,16,32]{2,1,0:T(8,128)(2,1)} %bitcast.14, s32[2,64]{1,0:T(2,128)} %bitcast.15, bf16[24,2,64]{2,1,0:T(2,128)(2,1)} %bitcast.13, ...), custom_call_target="tpu_custom_call" | custom-call | tf_op jit(solution)/shard_map/pallas_call | solution.py:506
  44.6 0.0 copy-start
  44.6 1.6 %copy.11 = f32[2,32,2,1,256]{4,3,2,1,0:T(1,128)} copy(f32[2,32,2,1,256]{4,3,2,1,0:T(1,128)} %bitcast.9) | data formatting | bytes 262144
  46.2 0.0 copy-done
  46.2 0.6 %copy.12 = f32[2,32,16]{1,2,0:T(8,128)} copy(f32[2,32,16]{1,2,0:T(8,128)S(1)} %bitcast.12) | data formatting | bytes 8192
Async XLA Ops:
  44.6 1.6 %copy-start = (f32[2,16,32]{2,1,0:T(8,128)S(1)}, f32[2,16,32]{2,1,0:T(8,128)}, u32[]{:S(2)}) copy-start(f32[2,16,32]{2,1,0:T(8,128)} %get-tuple-element.5) | copy-start | bytes 12292

commit v5 on v4

--- a/solution.py
+++ b/solution.py
@@ -49,8 +49,8 @@
     d_hbm,
     t_hbm,
     t2_hbm,
-    grad_hbm,
-    fg_hbm,
+    gout,
+    fo,
     bv,
     mv,
     lv,
@@ -81,11 +81,9 @@
     ea,
     zg,
     gv,
-    gout,
     gs,
     gz,
     gx,
-    fo,
     local,
     send,
     recv,
@@ -131,7 +129,13 @@
             src_ref=src, dst_ref=dst, send_sem=s, recv_sem=r, device_id=who, device_id_type=mesh_id
         )
 
-    everyone = [peer_ab(j) for j in range(1, nab)] + [peer_cf(j) for j in range(1, nc * nf)]
+    def far(j):
+        da, db = j // nb, j % nb
+        da, db = min(da, na - da), min(db, nb - db)
+        return (-da, -db, j)
+
+    others = sorted(range(1, nab), key=far)
+    everyone = [peer_ab(j) for j in others] + [peer_cf(j) for j in range(1, nc * nf)]
     barrier = pltpu.get_barrier_semaphore()
     for who in everyone:
         pl.semaphore_signal(barrier, inc=1, device_id=who, device_id_type=mesh_id)
@@ -187,7 +191,7 @@
         own_line = lg.at[ic, pl.ds(ab, 1)]
         remote(own_line, own_line, send.at[0], recv.at[0], peer_c(j)).start()
     for k in range(chunks):
-        for j in range(1, nab):
+        for j in others:
             to = lax.rem(ia + j // nb, na) * nb + lax.rem(ib + j % nb, nb)
             remote(
                 ht.at[k, to], hr.at[k, ab], send.at[1 + k], recv.at[1 + k], peer_ab(j)
@@ -214,7 +218,7 @@
 
     lax.fori_loop(0, chunks, again, 0)
     settle(lg.at[pl.ds(0, nc - 1), pl.ds(0, 1)], 0)
-    for j in range(1, nab):
+    for j in others:
         mine = lg.at[:, pl.ds(ab, 1)]
         remote(mine, mine, send.at[6], recv.at[6], peer_ab(j)).start()
     pair_rows = 2 * nc
@@ -335,7 +339,7 @@
         for j in range(1, nc):
             total = total + zr[k, j].astype(F32)
         ra[k, ab] = (total - kd[k]).astype(BF)
-        for j in range(1, nab):
+        for j in others:
             remote(
                 ra.at[k, ab], ra.at[k, ab], send.at[10 + k], recv.at[10 + k], peer_ab(j)
             ).start()
@@ -417,12 +421,10 @@
     for z in range(slab):
         for p in range(2):
             gout[p * rank : (p + 1) * rank, z] = out[2 * z + p].reshape(rank, 1, width)
-    store = pltpu.make_async_copy(gout, grad_hbm, local.at[7])
-    store.start()
 
     settle(gz.at[pl.ds(0, nc * nf - 1)], 13)
     gx[ab] = jnp.sum(gz[...].astype(F32), 0)
-    for j in range(1, nab):
+    for j in others:
         remote(gx.at[ab], gx.at[ab], send.at[14], recv.at[14], peer_ab(j)).start()
     settle(gx.at[pl.ds(0, nab - 1)], 14)
     total = jnp.sum(gx[...], 0)
@@ -430,10 +432,17 @@
         for h in range(2):
             at = (2 * h + q) * rank
             fo[q, h * half : (h + 1) * half, :] = total[:, at : at + rank]
-    last = pltpu.make_async_copy(fo, fg_hbm, local.at[8])
-    last.start()
-    last.wait()
-    store.wait()
+
+
+def finish(g_in, f_in, g_out, f_out, sems):
+    copies = [
+        pltpu.make_async_copy(g_in, g_out, sems.at[0]),
+        pltpu.make_async_copy(f_in, f_out, sems.at[1]),
+    ]
+    for copy in copies:
+        copy.start()
+    for copy in copies:
+        copy.wait()
 
 
 SHAPES = {64: (4, 4, 4), 8: (2, 2, 2)}
@@ -494,28 +503,37 @@
         vm((chunks, GROUP, width, 2 * lane), BF),
         vm((chunks, GROUP * sl, 2 * width), BF),
         vm((2 * sl, 2 * lane), F32),
-        vm((2 * rank, slab, 1, width), F32),
         vm((nf, span // 2, 4 * rank), BF),
         vm((nc * nf, span // 2, 4 * rank), BF),
         vm((nab, span // 2, 4 * rank), F32),
-        vm((2, span, rank), F32),
-        dma((9,)),
+        dma((7,)),
         dma((15,)),
         dma((15,)),
     ]
     grad, fg = pl.pallas_call(
         functools.partial(kernel, (na, nb, nc, nf, chunks), scale),
         out_shape=(
-            jax.ShapeDtypeStruct((2 * rank, slab, 1, width), F32),
-            jax.ShapeDtypeStruct((2, span, rank), F32),
+            pltpu.VMEM((2 * rank, slab, 1, width), F32),
+            pltpu.VMEM((2, span, rank), F32),
         ),
         in_specs=[pl.BlockSpec(memory_space=pl.ANY)] * 7,
-        out_specs=[pl.BlockSpec(memory_space=pl.ANY)] * 2,
+        out_specs=[pl.BlockSpec(memory_space=pltpu.VMEM)] * 2,
         scratch_shapes=scratch,
         compiler_params=pltpu.CompilerParams(
-            collective_id=0, has_side_effects=True, vmem_limit_bytes=56 * 1024 * 1024
+            collective_id=0, has_side_effects=True, vmem_limit_bytes=24 * 1024 * 1024
         ),
-    )(b, m, v, l, d, table, table2)
+    )(*[pltpu.with_memory_space_constraint(x, pltpu.HBM) for x in (b, m, v, l, d, table, table2)])
+    grad, fg = pl.pallas_call(
+        finish,
+        out_shape=(
+            jax.ShapeDtypeStruct(grad.shape, F32),
+            jax.ShapeDtypeStruct(fg.shape, F32),
+        ),
+        in_specs=[pl.BlockSpec(memory_space=pl.ANY)] * 2,
+        out_specs=[pl.BlockSpec(memory_space=pl.ANY)] * 2,
+        scratch_shapes=[dma((2,))],
+        compiler_params=pltpu.CompilerParams(vmem_limit_bytes=4 * 1024 * 1024),
+    )(grad, fg)
     return grad.reshape(basis.shape), fg.transpose(0, 2, 1)
 
 

time: 46.9 us -> 43.2 us (0.921)
  local copies, waits for them, and re-layouts: 2.18 us -> 0 us
  Pallas kernels: 44 us -> 42.4 us
    pallas_call x1, Pallas kernels: 44 us -> 41.8 us  [body(): pl.pallas_call(functools.partial(kernel, (na, nb, nc, nf, chunks), scale)...]
    unnamed x4 -> x0, local copies, waits for them, and re-layouts: 2.18 us -> none
    pallas_call x0 -> x1, Pallas kernels: none -> 0.68 us  [body(): pl.pallas_call(finish, out_shape=(jax.ShapeDtypeStruct(grad.shape, F32),...]
where the time goes in v5:
time: 43.2 us; the launch traced here: 43.1 us
  Pallas kernels  42.4 us (98%)
  between operations  0.64 us (1%)
    pallas_call x1, Pallas kernels, body(): pl.pallas_call(functools.partial(kernel, (na, nb, nc, nf, chunks), scale)...  41.8 us

profile of v5, /device:TPU:1, one launch (start us, length us, event | category | flops | bytes accessed | tf_op | source)
XLA Modules:
  0.0 43.1 jit_solution(10657801500478060644)
XLA Ops:
  0.6 41.8 %shard_map.86 = (f32[64,2,1,256]{3,2,1,0:T(1,128)S(1)}, f32[2,16,32]{2,1,0:T(8,128)S(1)}) custom-call(bf16[64,2,256]{2,1,0:T(2,128)(2,1)} %bitcast.9, bf16[24,2,256]{2,1,0:T(2,128)(2,1)} %bitcast.10, bf16[2,16,32]{2,1,0:T(8,128)(2,1)} %bitcast.12, s32[2,64]{1,0:T(2,128)} %bitcast.13, bf16[24,2,64]{2,1,0:T(2,128)(2,1)} %bitcast.11, ...), custom_call_target="tpu_custom_call" | custom-call | tf_op jit(solution)/shard_map/pallas_call | solution.py:513
  42.4 0.7 %shard_map.87 = (f32[64,2,1,256]{3,2,1,0:T(1,128)}, f32[2,16,32]{2,1,0:T(8,128)}) custom-call(f32[64,2,1,256]{3,2,1,0:T(1,128)S(1)} %get-tuple-element.6.g_in, f32[2,16,32]{2,1,0:T(8,128)S(1)} %get-tuple-element.7.f_in), custom_call_target="tpu_custom_call" | custom-call | tf_op jit(solution)/shard_map/pallas_call | solution.py:526

commit v6 on v5

--- a/solution.py
+++ b/solution.py
@@ -65,7 +65,6 @@
     img,
     ht,
     hr,
-    hn,
     vbt,
     vc,
     pf,
@@ -81,6 +80,8 @@
     ea,
     zg,
     gv,
+    hrt,
+    ef,
     gs,
     gz,
     gx,
@@ -208,15 +209,6 @@
     for j in range(1, nc):
         remote(kg.at[ic], kg.at[ic], send.at[5], recv.at[5], peer_c(j)).start()
     loads[6].wait()
-
-    def again(k, carry):
-        full = nt(img[k], t2_ref[...]).astype(BF)
-        for c4 in range(GROUP):
-            hn[k, c4, 0:sl, :] = full[c4 * sl : (c4 + 1) * sl, 0:width]
-            hn[k, c4, sl : 2 * sl, :] = full[c4 * sl : (c4 + 1) * sl, width : 2 * width]
-        return carry
-
-    lax.fori_loop(0, chunks, again, 0)
     settle(lg.at[pl.ds(0, nc - 1), pl.ds(0, 1)], 0)
     for j in others:
         mine = lg.at[:, pl.ds(ab, 1)]
@@ -278,15 +270,69 @@
     lo8 = iota((pair_rows, lane), 1) < frames
     top = iota((pair_rows, lane), 0) < nc
 
+    def hybrids(k, pair):
+        at = pair * 2 * sl
+        return jnp.concatenate(
+            [hr[k, :, p, :, at : at + 2 * sl].reshape(width, 2 * sl) for p in range(2)], 1
+        )
+
+    def residual(k):
+        settle(zr.at[k, pl.ds(0, nc - 1)], 7 + k)
+        total = zr[k, 0].astype(F32)
+        for j in range(1, nc):
+            total = total + zr[k, j].astype(F32)
+        ra[k, ab] = (total - kd[k]).astype(BF)
+
+    def gather(k):
+        for j in others:
+            remote(
+                ra.at[k, ab], ra.at[k, ab], send.at[10 + k], recv.at[10 + k], peer_ab(j)
+            ).start()
+
+    def factor_part(k):
+        whole = ra[k, ab].astype(F32)
+        for c4 in range(GROUP):
+            at = c4 // 2 * pair_rows
+            here = []
+            for q in range(2):
+                tile = whole[at : at + pair_rows, q * lane : (q + 1) * lane]
+                other = pltpu.roll(tile, nc, 0)
+                here.append(
+                    jnp.where(top, tile, other) if c4 % 2 == 0 else jnp.where(top, other, tile)
+                )
+            flip = [pltpu.roll(x, frames, 1) for x in here]
+            values = []
+            for s in range(2):
+                for a, b in zip(here, flip):
+                    x = jnp.where(lo8, a, b) if s == 0 else jnp.where(lo8, b, a)
+                    values.append((jnp.where(upper[s], 0.0, x), jnp.where(upper[s], x, 0.0)))
+            for i in range(nab):
+                p0, i0, p1, i1 = pf[0, 0, i], pf[0, 1, i], pf[1, 0, i], pf[1, 1, i]
+                re, im = [], []
+                for h in range(2):
+                    x0, y0, x1, y1 = [v[h] for v in values]
+                    re.append((p0 * x0 + i0 * y0) + (p1 * x1 + i1 * y1))
+                    im.append((p0 * y0 - i0 * x0) + (p1 * y1 - i1 * x1))
+                row = c4 * width + i * 2 * pair_rows
+                ef[row : row + 2 * pair_rows, 0:lane] = jnp.concatenate(re, 0).astype(BF)
+                ef[row : row + 2 * pair_rows, lane : 2 * lane] = jnp.concatenate(im, 0).astype(BF)
+        gv[...] += nn(hrt[k], ef[...])
+
+    def turn(k):
+        for p in range(2):
+            t = jnp.transpose(hr[k, :, p].reshape(width, GROUP * sl))
+            for c4 in range(GROUP):
+                hrt[k, p * sl : (p + 1) * sl, c4 * width : (c4 + 1) * width] = t[
+                    c4 * sl : (c4 + 1) * sl
+                ]
+
+    gv[...] = jnp.zeros_like(gv)
+
     def parts_of(k, carry):
         settle(hr.at[k, pl.ds(0, nab - 1)], 1 + k)
         tiles = []
         for pair in range(GROUP // 2):
-            at = pair * 2 * sl
-            lhs = jnp.concatenate(
-                [hr[k, :, p, :, at : at + 2 * sl].reshape(width, 2 * sl) for p in range(2)], 1
-            )
-            mixed = nt(lhs, vbt[...]).reshape(nab, ROWS * nc, 4 * lane)
+            mixed = nt(hybrids(k, pair), vbt[...]).reshape(nab, ROWS * nc, 4 * lane)
             totals = []
             for c2 in range(2):
                 re0, im0 = c2 * lane, (2 + c2) * lane
@@ -319,9 +365,18 @@
             remote(
                 zr.at[k, ic], zr.at[k, ic], send.at[7 + k], recv.at[7 + k], peer_c(j)
             ).start()
+        turn(k)
+
+        @pl.when(k >= 1)
+        def _():
+            residual(k - 1)
+            factor_part(k - 1)
+
         return carry
 
     lax.fori_loop(0, chunks, parts_of, 0)
+    for k in range(chunks - 1):
+        gather(k)
     settle(lg.at[:, pl.ds(0, nab - 1)], 6)
     lo = iota((blocks, lane), 1) < frames
     both = lg[...].reshape(blocks, lane)
@@ -333,44 +388,9 @@
         angle = lax.rem(kz * zpos, depth).astype(F32) * (2.0 * math.pi / depth)
         ph[s, 0] = (jnp.cos(angle) * norm).astype(BF).astype(F32)
         ph[s, 1] = (jnp.sin(angle) * -norm).astype(BF).astype(F32)
-    for k in range(chunks):
-        settle(zr.at[k, pl.ds(0, nc - 1)], 7 + k)
-        total = zr[k, 0].astype(F32)
-        for j in range(1, nc):
-            total = total + zr[k, j].astype(F32)
-        ra[k, ab] = (total - kd[k]).astype(BF)
-        for j in others:
-            remote(
-                ra.at[k, ab], ra.at[k, ab], send.at[10 + k], recv.at[10 + k], peer_ab(j)
-            ).start()
-    gv[...] = jnp.zeros_like(gv)
-
-    def spread(k, carry):
-        settle(ra.at[k, pl.ds(0, nab - 1)], 10 + k)
-        resid = nn(permt[...], ra[k].reshape(n_rows, 2 * lane))
-        for c4 in range(GROUP):
-            here = [
-                resid[c4 * blocks : (c4 + 1) * blocks, q * lane : (q + 1) * lane] for q in range(2)
-            ]
-            flip = [pltpu.roll(x, frames, 1) for x in here]
-            terms = []
-            for s in range(2):
-                xr_, xi_ = [
-                    jnp.where(lo, a, b) if s == 0 else jnp.where(lo, b, a)
-                    for a, b in zip(here, flip)
-                ]
-                pr, pi = ph[s, 0], ph[s, 1]
-                terms.append((xr_ * pr + xi_ * pi, xi_ * pr - xr_ * pi))
-            for r in range(ROWS):
-                m0, m1 = rowid[0] == r, rowid[1] == r
-                for q in range(2):
-                    ea[k, c4, r * blocks : (r + 1) * blocks, q * lane : (q + 1) * lane] = (
-                        jnp.where(m0, terms[0][q], 0.0) + jnp.where(m1, terms[1][q], 0.0)
-                    ).astype(BF)
-            gv[...] += nn(hn[k, c4], ea[k, c4])
-        return carry
-
-    lax.fori_loop(0, chunks, spread, 0)
+    residual(chunks - 1)
+    gather(chunks - 1)
+    factor_part(chunks - 1)
 
     own = {}
     for p in range(2):
@@ -395,6 +415,36 @@
         remote(
             gs.at[lax.rem(fr + j % nf, nf)], gz.at[spot_cf], send.at[13], recv.at[13], peer_cf(j)
         ).start()
+    def spread(k, carry):
+        settle(ra.at[k, pl.ds(0, nab - 1)], 10 + k)
+        resid = nn(permt[...], ra[k].reshape(n_rows, 2 * lane))
+        for c4 in range(GROUP):
+            here = [
+                resid[c4 * blocks : (c4 + 1) * blocks, q * lane : (q + 1) * lane] for q in range(2)
+            ]
+            flip = [pltpu.roll(x, frames, 1) for x in here]
+            terms = []
+            for s in range(2):
+                xr_, xi_ = [
+                    jnp.where(lo, a, b) if s == 0 else jnp.where(lo, b, a)
+                    for a, b in zip(here, flip)
+                ]
+                pr, pi = ph[s, 0], ph[s, 1]
+                terms.append((xr_ * pr + xi_ * pi, xi_ * pr - xr_ * pi))
+            for r in range(ROWS):
+                m0, m1 = rowid[0] == r, rowid[1] == r
+                for q in range(2):
+                    ea[k, c4, r * blocks : (r + 1) * blocks, q * lane : (q + 1) * lane] = (
+                        jnp.where(m0, terms[0][q], 0.0) + jnp.where(m1, terms[1][q], 0.0)
+                    ).astype(BF)
+        return carry
+
+    lax.fori_loop(0, chunks, spread, 0)
+
+    settle(gz.at[pl.ds(0, nc * nf - 1)], 13)
+    gx[ab] = jnp.sum(gz[...].astype(F32), 0)
+    for j in others:
+        remote(gx.at[ab], gx.at[ab], send.at[14], recv.at[14], peer_ab(j)).start()
 
     def backward(k, carry):
         for c4 in range(GROUP):
@@ -421,11 +471,6 @@
     for z in range(slab):
         for p in range(2):
             gout[p * rank : (p + 1) * rank, z] = out[2 * z + p].reshape(rank, 1, width)
-
-    settle(gz.at[pl.ds(0, nc * nf - 1)], 13)
-    gx[ab] = jnp.sum(gz[...].astype(F32), 0)
-    for j in others:
-        remote(gx.at[ab], gx.at[ab], send.at[14], recv.at[14], peer_ab(j)).start()
     settle(gx.at[pl.ds(0, nab - 1)], 14)
     total = jnp.sum(gx[...], 0)
     for q in range(2):
@@ -487,7 +532,6 @@
         vm((chunks, GROUP * sl, 2 * width), BF),
         vm((chunks, nab, 2, ROWS * nc, GROUP * sl), BF),
         vm((chunks, nab, 2, ROWS * nc, GROUP * sl), BF),
-        vm((chunks, GROUP, 2 * sl, width), BF),
         vm((8 * frames, 8 * rank), BF),
         vm((2 * sl, 2 * lane), BF),
         vm((2, 2, nab, 2 * nc, lane), F32),
@@ -503,6 +547,8 @@
         vm((chunks, GROUP, width, 2 * lane), BF),
         vm((chunks, GROUP * sl, 2 * width), BF),
         vm((2 * sl, 2 * lane), F32),
+        vm((chunks, 2 * sl, GROUP * width), BF),
+        vm((GROUP * width, 2 * lane), BF),
         vm((nf, span // 2, 4 * rank), BF),
         vm((nc * nf, span // 2, 4 * rank), BF),
         vm((nab, span // 2, 4 * rank), F32),

time: 43.2 us -> 40.2 us (0.931)
  Pallas kernels: 42.4 us -> 39.5 us
    pallas_call x1, Pallas kernels: 41.8 us -> 38.8 us  [body(): pl.pallas_call(functools.partial(kernel, (na, nb, nc, nf, chunks), scale)...]
where the time goes in v6:
time: 40.2 us; the launch traced here: 40.1 us
  Pallas kernels  39.5 us (98%)
  between operations  0.64 us (2%)
    pallas_call x1, Pallas kernels, body(): pl.pallas_call(functools.partial(kernel, (na, nb, nc, nf, chunks), scale)...  38.8 us

profile of v6, /device:TPU:1, one launch (start us, length us, event | category | flops | bytes accessed | tf_op | source)
XLA Modules:
  0.0 40.1 jit_solution(17749805498188671251)
XLA Ops:
  0.6 38.8 %shard_map.86 = (f32[64,2,1,256]{3,2,1,0:T(1,128)S(1)}, f32[2,16,32]{2,1,0:T(8,128)S(1)}) custom-call(bf16[64,2,256]{2,1,0:T(2,128)(2,1)} %bitcast.9, bf16[24,2,256]{2,1,0:T(2,128)(2,1)} %bitcast.10, bf16[2,16,32]{2,1,0:T(8,128)(2,1)} %bitcast.12, s32[2,64]{1,0:T(2,128)} %bitcast.13, bf16[24,2,64]{2,1,0:T(2,128)(2,1)} %bitcast.11, ...), custom_call_target="tpu_custom_call" | custom-call | tf_op jit(solution)/shard_map/pallas_call | solution.py:559
  39.4 0.7 %shard_map.87 = (f32[64,2,1,256]{3,2,1,0:T(1,128)}, f32[2,16,32]{2,1,0:T(8,128)}) custom-call(f32[64,2,1,256]{3,2,1,0:T(1,128)S(1)} %get-tuple-element.6.g_in, f32[2,16,32]{2,1,0:T(8,128)S(1)} %get-tuple-element.7.f_in), custom_call_target="tpu_custom_call" | custom-call | tf_op jit(solution)/shard_map/pallas_call | solution.py:572

commit v7 on v6

--- a/solution.py
+++ b/solution.py
@@ -82,6 +82,7 @@
     gv,
     hrt,
     ef,
+    mx,
     gs,
     gz,
     gx,
@@ -191,12 +192,20 @@
     for j in range(1, nc):
         own_line = lg.at[ic, pl.ds(ab, 1)]
         remote(own_line, own_line, send.at[0], recv.at[0], peer_c(j)).start()
-    for k in range(chunks):
+    def exchange(k):
         for j in others:
             to = lax.rem(ia + j // nb, na) * nb + lax.rem(ib + j % nb, nb)
             remote(
                 ht.at[k, to], hr.at[k, ab], send.at[1 + k], recv.at[1 + k], peer_ab(j)
             ).start()
+
+    exchange(0)
+
+    @pl.when(lax.rem(fr, 2) == 0)
+    def _():
+        for k in range(1, chunks):
+            exchange(k)
+
     for j in range(1, nf):
         remote(vg.at[fr], vg.at[fr], send.at[4], recv.at[4], peer_f(j)).start()
     loads[5].wait()
@@ -213,6 +222,12 @@
     for j in others:
         mine = lg.at[:, pl.ds(ab, 1)]
         remote(mine, mine, send.at[6], recv.at[6], peer_ab(j)).start()
+
+    @pl.when(lax.rem(fr, 2) == 1)
+    def _():
+        for k in range(1, chunks):
+            exchange(k)
+
     pair_rows = 2 * nc
     l8[0:nc] = lg[:, ab]
     l8[nc:pair_rows] = lg[:, ab]
@@ -332,28 +347,36 @@
         settle(hr.at[k, pl.ds(0, nab - 1)], 1 + k)
         tiles = []
         for pair in range(GROUP // 2):
-            mixed = nt(hybrids(k, pair), vbt[...]).reshape(nab, ROWS * nc, 4 * lane)
+            mx[pair] = nt(hybrids(k, pair), vbt[...])
+        for pair in range(GROUP // 2):
+            got = [[[0.0, 0.0], [0.0, 0.0]], [[0.0, 0.0], [0.0, 0.0]]]
+            for i in range(nab):
+                row = i * 2 * pair_rows
+                phase = [[pf[s, q, i] for q in range(2)] for s in range(2)]
+                for c2 in range(2):
+                    low, high = [
+                        [
+                            mx[
+                                pair,
+                                row + h * pair_rows : row + (h + 1) * pair_rows,
+                                (2 * q + c2) * lane : (2 * q + c2 + 1) * lane,
+                            ]
+                            for q in range(2)
+                        ]
+                        for h in range(2)
+                    ]
+                    for s in range(2):
+                        mr = jnp.where(upper[s], high[0], low[0])
+                        mi = jnp.where(upper[s], high[1], low[1])
+                        pr, pi = phase[s]
+                        got[c2][s][0] = got[c2][s][0] + (pr * mr - pi * mi)
+                        got[c2][s][1] = got[c2][s][1] + (pr * mi + pi * mr)
             totals = []
             for c2 in range(2):
-                re0, im0 = c2 * lane, (2 + c2) * lane
-                got = []
-                for s in range(2):
-                    mr = jnp.where(
-                        upper[s][None],
-                        mixed[:, pair_rows:, re0 : re0 + lane],
-                        mixed[:, :pair_rows, re0 : re0 + lane],
-                    )
-                    mi = jnp.where(
-                        upper[s][None],
-                        mixed[:, pair_rows:, im0 : im0 + lane],
-                        mixed[:, :pair_rows, im0 : im0 + lane],
-                    )
-                    pr, pi = pf[s, 0], pf[s, 1]
-                    got.append((jnp.sum(pr * mr - pi * mi, 0), jnp.sum(pr * mi + pi * mr, 0)))
                 both_q = []
                 for q in range(2):
-                    keep = jnp.where(lo8, got[0][q], got[1][q])
-                    fold = jnp.where(lo8, got[1][q], got[0][q])
+                    keep = jnp.where(lo8, got[c2][0][q], got[c2][1][q])
+                    fold = jnp.where(lo8, got[c2][1][q], got[c2][0][q])
                     total = keep + pltpu.roll(fold, frames, 1)
                     both_q.append(total + pltpu.roll(total, nc, 0))
                 totals.append(both_q)
@@ -416,6 +439,13 @@
             gs.at[lax.rem(fr + j % nf, nf)], gz.at[spot_cf], send.at[13], recv.at[13], peer_cf(j)
         ).start()
     def spread(k, carry):
+        @pl.when(k == chunks - 1)
+        def _():
+            settle(gz.at[pl.ds(0, nc * nf - 1)], 13)
+            gx[ab] = jnp.sum(gz[...].astype(F32), 0)
+            for j in others:
+                remote(gx.at[ab], gx.at[ab], send.at[14], recv.at[14], peer_ab(j)).start()
+
         settle(ra.at[k, pl.ds(0, nab - 1)], 10 + k)
         resid = nn(permt[...], ra[k].reshape(n_rows, 2 * lane))
         for c4 in range(GROUP):
@@ -440,11 +470,6 @@
         return carry
 
     lax.fori_loop(0, chunks, spread, 0)
-
-    settle(gz.at[pl.ds(0, nc * nf - 1)], 13)
-    gx[ab] = jnp.sum(gz[...].astype(F32), 0)
-    for j in others:
-        remote(gx.at[ab], gx.at[ab], send.at[14], recv.at[14], peer_ab(j)).start()
 
     def backward(k, carry):
         for c4 in range(GROUP):
@@ -549,6 +574,7 @@
         vm((2 * sl, 2 * lane), F32),
         vm((chunks, 2 * sl, GROUP * width), BF),
         vm((GROUP * width, 2 * lane), BF),
+        vm((2, width, 4 * lane), F32),
         vm((nf, span // 2, 4 * rank), BF),
         vm((nc * nf, span // 2, 4 * rank), BF),
         vm((nab, span // 2, 4 * rank), F32),

time: 40.2 us -> 37.2 us (0.925)
  Pallas kernels: 39.5 us -> 36.5 us
    pallas_call x1, Pallas kernels: 38.8 us -> 35.8 us  [body(): pl.pallas_call(functools.partial(kernel, (na, nb, nc, nf, chunks), scale)...]
where the time goes in v7:
time: 37.2 us; the launch traced here: 37.1 us
  Pallas kernels  36.5 us (98%)
  between operations  0.64 us (2%)
    pallas_call x1, Pallas kernels, body(): pl.pallas_call(functools.partial(kernel, (na, nb, nc, nf, chunks), scale)...  35.8 us

profile of v7, /device:TPU:1, one launch (start us, length us, event | category | flops | bytes accessed | tf_op | source)
XLA Modules:
  0.0 37.1 jit_solution(3578181507251643495)
XLA Ops:
  0.6 35.8 %shard_map.86 = (f32[64,2,1,256]{3,2,1,0:T(1,128)S(1)}, f32[2,16,32]{2,1,0:T(8,128)S(1)}) custom-call(bf16[64,2,256]{2,1,0:T(2,128)(2,1)} %bitcast.9, bf16[24,2,256]{2,1,0:T(2,128)(2,1)} %bitcast.10, bf16[2,16,32]{2,1,0:T(8,128)(2,1)} %bitcast.12, s32[2,64]{1,0:T(2,128)} %bitcast.13, bf16[24,2,64]{2,1,0:T(2,128)(2,1)} %bitcast.11, ...), custom_call_target="tpu_custom_call" | custom-call | tf_op jit(solution)/shard_map/pallas_call | solution.py:585
  36.5 0.7 %shard_map.87 = (f32[64,2,1,256]{3,2,1,0:T(1,128)}, f32[2,16,32]{2,1,0:T(8,128)}) custom-call(f32[64,2,1,256]{3,2,1,0:T(1,128)S(1)} %get-tuple-element.6.g_in, f32[2,16,32]{2,1,0:T(8,128)S(1)} %get-tuple-element.7.f_in), custom_call_target="tpu_custom_call" | custom-call | tf_op jit(solution)/shard_map/pallas_call | solution.py:598

commit v8 on v7

--- a/solution.py
+++ b/solution.py
@@ -193,7 +193,7 @@
         own_line = lg.at[ic, pl.ds(ab, 1)]
         remote(own_line, own_line, send.at[0], recv.at[0], peer_c(j)).start()
     def exchange(k):
-        for j in others:
+        for j in sorted(others, key=lambda j: (far(j)[0] + far(j)[1], j * 7 % nab)):
             to = lax.rem(ia + j // nb, na) * nb + lax.rem(ib + j % nb, nb)
             remote(
                 ht.at[k, to], hr.at[k, ab], send.at[1 + k], recv.at[1 + k], peer_ab(j)

time: 37.2 us -> 37.6 us (1.011)
  no operation moved by 1% of the time
where the time goes in v8:
time: 37.6 us; the launch traced here: 37.5 us
  Pallas kernels  36.8 us (98%)
  between operations  0.64 us (2%)
    pallas_call x1, Pallas kernels, body(): pl.pallas_call(functools.partial(kernel, (na, nb, nc, nf, chunks), scale)...  36.2 us

profile of v8, /device:TPU:1, one launch (start us, length us, event | category | flops | bytes accessed | tf_op | source)
XLA Modules:
  0.0 37.5 jit_solution(6968750565800444369)
XLA Ops:
  0.6 36.2 %shard_map.86 = (f32[64,2,1,256]{3,2,1,0:T(1,128)S(1)}, f32[2,16,32]{2,1,0:T(8,128)S(1)}) custom-call(bf16[64,2,256]{2,1,0:T(2,128)(2,1)} %bitcast.9, bf16[24,2,256]{2,1,0:T(2,128)(2,1)} %bitcast.10, bf16[2,16,32]{2,1,0:T(8,128)(2,1)} %bitcast.12, s32[2,64]{1,0:T(2,128)} %bitcast.13, bf16[24,2,64]{2,1,0:T(2,128)(2,1)} %bitcast.11, ...), custom_call_target="tpu_custom_call" | custom-call | tf_op jit(solution)/shard_map/pallas_call | solution.py:585
  36.8 0.7 %shard_map.87 = (f32[64,2,1,256]{3,2,1,0:T(1,128)}, f32[2,16,32]{2,1,0:T(8,128)}) custom-call(f32[64,2,1,256]{3,2,1,0:T(1,128)S(1)} %get-tuple-element.6.g_in, f32[2,16,32]{2,1,0:T(8,128)S(1)} %get-tuple-element.7.f_in), custom_call_target="tpu_custom_call" | custom-call | tf_op jit(solution)/shard_map/pallas_call | solution.py:598
